TPU v7x, 32 devices: a whole 2x2x4 slice. The times are simulated.
32 devices in a mesh: fsdp: 16 (over z, x, core), dp: 2 (over y).
Axes of the slice: x: 2, y: 2, z: 4, core: 2. Of those that a mesh axis runs over, the one named last changes fastest.
Arguments:
- tokens: bfloat16 [4096, 4096], P(('fsdp', 'dp')), may hold values from -6 to 6
- owner: int32 [4096, 4], P(('fsdp', 'dp')), may hold values from 0 to 15, all different within a row; in each aligned block of 128 rows (0 to 127, 128 to 255, ...) at most 48 rows name the same one
- row_pick: int32 [4096, 4, 32], P(('fsdp', 'dp')), may hold values from 0 to 255, as said below
- query_weight: bfloat16 [4096, 512], P('fsdp'), may hold values from -0.09375 to 0.09375
- sub_keys: bfloat16 [4, 256, 128], replicated, may hold values from -2000 to 2000
- values: bfloat16 [4096, 4096], P('fsdp'), may hold values from -6 to 6
- cotangent: bfloat16 [4096, 4096], P(('fsdp', 'dp')), may hold values from -6 to 6
Outputs:
- memory_out: bfloat16 [4096, 4096], P(('fsdp', 'dp'))
- grad_values: bfloat16 [4096, 4096], P(('fsdp', 'dp'))
Inputs may be any that keep to these rules, and one draw needn't show every extreme that they name: `owner`: each token's 4 heads name different blocks; the 128 tokens of one device name no block more than 48 times, and some block exactly 48 times. `row_pick`: the 32 rows that one head of one token reads are distinct.
All inputs are finite; a program needn't handle non-finite values.
Results may differ from a plain program's by a relative error of at most 0.012.
The roundings to bfloat16 on the way count: a program that leaves them out, or rounds other values in their place, can miss the bound.
Values may be sent and summed in bfloat16 or wider, within the bound.
A program may use at most 64 MiB of HBM per device.

v0:
```python
import jax
import jax.numpy as jnp
from jax import lax
from jax.sharding import PartitionSpec as P


def body(tokens, owner, row_pick, query_weight, sub_keys, values, cotangent):
    tok_rows = tokens.shape[0]
    heads = owner.shape[1]
    width = tokens.shape[1]
    block_rows = values.shape[0]
    key_width = sub_keys.shape[2]
    groups = lax.axis_size("fsdp")
    capacity = max(2, 3 * tok_rows * heads // (2 * groups))
    total_slots = groups * capacity
    requests = tok_rows * heads
    columns = tokens
    query = jnp.dot(
        columns,
        lax.all_gather(query_weight, "fsdp", axis=0, tiled=True),
        preferred_element_type=jnp.float32,
    ).astype(jnp.bfloat16)
    query = query.reshape(tok_rows, heads, key_width)
    full = jnp.einsum("thk,hrk->thr", query, sub_keys, preferred_element_type=jnp.float32)
    match = row_pick[:, :, :, None] == jnp.arange(block_rows, dtype=jnp.int32)[None, None, None, :]
    picked = jnp.sum(jnp.where(match, full[:, :, None, :], 0.0), axis=3)
    score = picked * (1.0 / key_width**0.5)
    top = jnp.max(score, axis=2, keepdims=True)
    expo = jnp.exp(score - top)
    weight = (expo / jnp.sum(expo, axis=2, keepdims=True)).astype(jnp.bfloat16)
    table = jnp.sum(jnp.where(match, weight.astype(jnp.float32)[:, :, :, None], 0.0), axis=2)
    table = table.astype(jnp.bfloat16).reshape(requests, block_rows)
    flat_owner = owner.reshape(-1)
    hits = (flat_owner[:, None] == jnp.arange(groups, dtype=jnp.int32)[None, :]).astype(jnp.float32)
    positions = jnp.arange(requests, dtype=jnp.int32)
    lower = (positions[:, None] >= positions[None, :]).astype(jnp.float32)
    counts = jnp.dot(
        lower, hits, precision=lax.Precision.HIGHEST, preferred_element_type=jnp.float32
    )
    ranks = jnp.sum((counts - 1.0) * hits, axis=1).astype(jnp.int32)
    slot = flat_owner * capacity + ranks
    dispatch = (jnp.arange(total_slots, dtype=jnp.int32)[:, None] == slot[None, :]).astype(
        jnp.bfloat16
    )
    table_send = jnp.dot(dispatch, table, preferred_element_type=jnp.float32).astype(jnp.bfloat16)
    table_send = table_send.reshape(groups, capacity, block_rows)
    per_token = jnp.sum(
        dispatch.astype(jnp.float32).reshape(total_slots, tok_rows, heads), axis=2
    ).astype(jnp.bfloat16)
    grad_send = jnp.dot(per_token, cotangent, preferred_element_type=jnp.float32).astype(
        jnp.bfloat16
    )
    grad_send = grad_send.reshape(groups, capacity, width)
    table_recv, grad_recv = (
        lax.all_to_all(table_send, "fsdp", split_axis=0, concat_axis=0, tiled=True),
        lax.all_to_all(grad_send, "fsdp", split_axis=0, concat_axis=0, tiled=True),
    )
    table_flat = table_recv.reshape(total_slots, block_rows)
    grad_flat = grad_recv.reshape(total_slots, width)
    columns = table_flat
    grad_values = lax.psum_scatter(
        lax.dot_general(
            columns, grad_flat, (((0,), (0,)), ((), ())), preferred_element_type=jnp.float32
        ),
        "dp",
        scatter_dimension=0,
        tiled=True,
    ).astype(jnp.bfloat16)
    partial_value = jnp.dot(
        table_recv.reshape(-1, block_rows), values, preferred_element_type=jnp.float32
    )
    partial_value = partial_value.astype(jnp.bfloat16).reshape(
        table_recv.shape[0], table_recv.shape[1], width
    )
    readback = lax.all_to_all(partial_value, "fsdp", split_axis=0, concat_axis=0, tiled=True)
    readback_flat = readback.reshape(total_slots, width)
    memory_out = lax.dot_general(
        per_token, readback_flat, (((0,), (0,)), ((), ())), preferred_element_type=jnp.float32
    )
    return (memory_out.astype(jnp.bfloat16), grad_values)


def solution(mesh):
    placed = (
        P(("fsdp", "dp"), None),
        P(("fsdp", "dp"), None),
        P(("fsdp", "dp"), None, None),
        P("fsdp", None),
        P(),
        P("fsdp", None),
        P(("fsdp", "dp"), None),
    )
    return jax.shard_map(
        body,
        mesh=mesh,
        in_specs=placed,
        out_specs=(P(("fsdp", "dp"), None), P(("fsdp", "dp"), None)),
        check_vma=False,
    )
```

profile of v0, /device:TPU:11, one launch (start us, length us, event | category | flops | bytes accessed | tf_op | source)
XLA Modules:
  0.0 391.2 jit_solution(17401417014841593466)
XLA Ops:
  7.2 0.7 all-gather.2.cloned.1.call-update
  7.9 0.8 copy.30
  8.8 1.0 copy.32
  9.8 0.3 fusion.12
  10.3 51.0 %all-gather.2.cloned.1.call-done = bf16[4096,512]{1,0:T(8,128)(2,1)} async-done(((bf16[256,512]{1,0:T(8,128)(2,1)}), bf16[4096,512]{1,0:T(8,128)(2,1)}) %all-gather.2.cloned.1.call-update) | async-done | bytes 4194320 | tf_op jit(solution)/shard_map/all_gather | solution.py:20
  61.2 3.2 fusion.5
  64.5 0.2 convolution_bitcast_fusion.1
  64.7 0.3 copy.34
  65.1 5.3 %select_reduce_fusion.1 = f32[128,4,32]{2,1,0:T(4,128)S(1)} fusion(f32[128,4,256]{2,1,0:T(4,128)S(1)} %copy.34, s32[128,4,32]{2,1,0:T(4,128)S(1)} %copy.32), kind=kLoop, calls=%fused_computation.3 | loop fusion | flops 12566528 | bytes 655360 | tf_op jit(solution)/shard_map/reduce_sum | solution.py:26
  70.7 6.6 %select_reduce_fusion = bf16[128,4,256]{2,1,0:T(4,128)(2,1)S(1)} fusion(f32[128,4,32]{2,1,0:T(4,128)S(1)} %copy.36, s32[128,4,32]{2,1,0:T(4,128)S(1)} %copy.32), kind=kLoop, calls=%fused_computation.2 | loop fusion | flops 12451840 | bytes 393216 | tf_op jit(solution)/shard_map/reduce_sum | solution.py:31
  77.4 1.2 fusion.4
  78.5 4.7 %all-to-all-start = ((bf16[16,48,256]{2,1,0:T(8,128)(2,1)}), bf16[16,48,256]{2,1,0:T(8,128)(2,1)S(1)}, u32[]{:S(2)}, u32[]{:S(2)}) async-start(bf16[16,48,256]{2,1,0:T(8,128)(2,1)} %bitcast.1), calls=%async_computation | async-start | bytes 786432 | tf_op jit(solution)/shard_map/all_to_all | solution.py:55
  83.2 0.2 fusion.13
  83.4 5.7 %convolution_convert_fusion = bf16[768,4096]{1,0:T(8,128)(2,1)} fusion(bf16[768,128]{1,0:T(8,128)(2,1)S(1)} %fusion.13, bf16[128,4096]{1,0:T(8,128)(2,1)} %param.13), kind=kOutput, calls=%fused_computation.5 | convolution fusion | flops 808452096 | bytes 7536640 | tf_op jit(solution)/shard_map/dot_general | solution.py:50
  89.1 4.9 %all-to-all-done = bf16[16,48,256]{2,1,0:T(8,128)(2,1)S(1)} async-done(((bf16[16,48,256]{2,1,0:T(8,128)(2,1)}), bf16[16,48,256]{2,1,0:T(8,128)(2,1)S(1)}, u32[]{:S(2)}, u32[]{:S(2)}) %all-to-all-start) | async-done | bytes 393248 | tf_op jit(solution)/shard_map/all_to_all | solution.py:55
  94.0 6.0 %all-to-all-start.2 = ((bf16[16,48,4096]{2,1,0:T(8,128)(2,1)}), bf16[16,48,4096]{2,1,0:T(8,128)(2,1)}, u32[]{:S(2)}, u32[]{:S(2)}) async-start(bf16[16,48,4096]{2,1,0:T(8,128)(2,1)} %bitcast.26), calls=%async_computation.2 | async-start | bytes 12582912 | tf_op jit(solution)/shard_map/all_to_all | solution.py:56
  100.0 4.5 %convolution_convert_fusion.1 = bf16[768,4096]{1,0:T(8,128)(2,1)} fusion(bf16[768,256]{1,0:T(8,128)(2,1)S(1)} %bitcast.28, bf16[256,4096]{1,0:T(8,128)(2,1)S(1)} %copy-done), kind=kOutput, calls=%fused_computation.6 | convolution fusion | flops 1613758464 | bytes 8781824 | tf_op jit(solution)/shard_map/dot_general | solution.py:69
  104.4 133.0 %all-to-all-done.2 = bf16[16,48,4096]{2,1,0:T(8,128)(2,1)} async-done(((bf16[16,48,4096]{2,1,0:T(8,128)(2,1)}), bf16[16,48,4096]{2,1,0:T(8,128)(2,1)}, u32[]{:S(2)}, u32[]{:S(2)}) %all-to-all-start.2) | async-done | bytes 6291488 | tf_op jit(solution)/shard_map/all_to_all | solution.py:56
  237.4 4.8 %all-to-all-start.1 = ((bf16[16,48,4096]{2,1,0:T(8,128)(2,1)}), bf16[16,48,4096]{2,1,0:T(8,128)(2,1)}, u32[]{:S(2)}, u32[]{:S(2)}) async-start(bf16[16,48,4096]{2,1,0:T(8,128)(2,1)} %bitcast.27), calls=%async_computation.1 | async-start | bytes 12582912 | tf_op jit(solution)/shard_map/all_to_all | solution.py:75
  242.2 6.6 %convolution_bitcast_fusion = f32[256,4096]{1,0:T(8,128)} fusion(bf16[16,48,256]{2,1,0:T(8,128)(2,1)S(1)} %all-to-all-done, bf16[16,48,4096]{2,1,0:T(8,128)(2,1)} %all-to-all-done.2), kind=kOutput, calls=%fused_computation.7 | convolution fusion | flops 1610612736 | bytes 10878976 | tf_op jit(solution)/shard_map/dot_general | solution.py:62
  248.9 55.0 %reduce-scatter.2.cloned.1.call-done = f32[128,4096]{1,0:T(8,128)} async-done(((f32[256,4096]{1,0:T(8,128)}), f32[128,4096]{1,0:T(8,128)}) %reduce-scatter.2.cloned.1.call-update) | async-done | bytes 2097168 | tf_op jit(solution)/shard_map/reduce_scatter | solution.py:61
  303.8 2.7 convert_element_type.71
  306.5 73.0 %all-to-all-done.1 = bf16[16,48,4096]{2,1,0:T(8,128)(2,1)} async-done(((bf16[16,48,4096]{2,1,0:T(8,128)(2,1)}), bf16[16,48,4096]{2,1,0:T(8,128)(2,1)}, u32[]{:S(2)}, u32[]{:S(2)}) %all-to-all-start.1) | async-done | bytes 6291488 | tf_op jit(solution)/shard_map/all_to_all | solution.py:75
  379.5 4.8 %convolution_convert_fusion.2 = bf16[128,4096]{1,0:T(8,128)(2,1)} fusion(bf16[768,128]{1,0:T(8,128)(2,1)S(1)} %fusion.13, bf16[768,4096]{1,0:T(8,128)(2,1)} %bitcast.4), kind=kOutput, calls=%fused_computation.8 | convolution fusion | flops 805830656 | bytes 7536640 | tf_op jit(solution)/shard_map/dot_general | solution.py:77
  (19 shorter events, 0.8 us)
Async XLA Ops:
  7.2 92.8 %copy-start = (bf16[256,4096]{1,0:T(8,128)(2,1)S(1)}, bf16[256,4096]{1,0:T(8,128)(2,1)}, u32[]{:S(2)}) copy-start(bf16[256,4096]{1,0:T(8,128)(2,1)} %param.12) | copy-start | bytes 6291460
  7.2 57.3 %copy-start.1 = (bf16[4,256,128]{2,1,0:T(8,128)(2,1)S(1)}, bf16[4,256,128]{2,1,0:T(8,128)(2,1)}, u32[]{:S(2)}) copy-start(bf16[4,256,128]{2,1,0:T(8,128)(2,1)} %param.11) | copy-start | bytes 786436
  7.2 54.1 %all-gather.2.cloned.1.call-start = ((), (), s32[]{:S(2)}) async-start(), calls=%async_computation.4 | async-start | bytes 4456448 | tf_op jit(solution)/shard_map/all_gather | solution.py:20
  10.3 72.9 %copy-start.2 = (s32[128,4]{0,1:T(4,128)S(1)}, s32[128,4]{0,1:T(4,128)}, u32[]{:S(2)}) copy-start(s32[128,4]{0,1:T(4,128)} %param.8) | copy-start | bytes 6148
  78.5 15.4 %all-to-all-start = ((bf16[16,48,256]{2,1,0:T(8,128)(2,1)}), bf16[16,48,256]{2,1,0:T(8,128)(2,1)S(1)}, u32[]{:S(2)}, u32[]{:S(2)}) async-start(bf16[16,48,256]{2,1,0:T(8,128)(2,1)} %bitcast.1), calls=%async_computation | async-start | bytes 786432 | tf_op jit(solution)/shard_map/all_to_all | solution.py:55
  94.0 143.4 %all-to-all-start.2 = ((bf16[16,48,4096]{2,1,0:T(8,128)(2,1)}), bf16[16,48,4096]{2,1,0:T(8,128)(2,1)}, u32[]{:S(2)}, u32[]{:S(2)}) async-start(bf16[16,48,4096]{2,1,0:T(8,128)(2,1)} %bitcast.26), calls=%async_computation.2 | async-start | bytes 12582912 | tf_op jit(solution)/shard_map/all_to_all | solution.py:56
  237.4 142.2 %all-to-all-start.1 = ((bf16[16,48,4096]{2,1,0:T(8,128)(2,1)}), bf16[16,48,4096]{2,1,0:T(8,128)(2,1)}, u32[]{:S(2)}, u32[]{:S(2)}) async-start(bf16[16,48,4096]{2,1,0:T(8,128)(2,1)} %bitcast.27), calls=%async_computation.1 | async-start | bytes 12582912 | tf_op jit(solution)/shard_map/all_to_all | solution.py:75
  242.1 61.7 %reduce-scatter.2.cloned.1.call-start = ((), (), s32[]{:S(2)}) async-start(), calls=%async_computation.5 | async-start | bytes 6291456 | tf_op jit(solution)/shard_map/reduce_scatter | solution.py:61
Sparse Core Ops, SparseCore 0:
  10.2 51.0 all-gather.1
  249.0 54.7 reduce-scatter.1
where the time goes:
time: 392 us; the launch traced here: 391 us
  waiting for transfers between devices  318 us (81%)
  matrix products  26.4 us (7%)
  starting transfers between devices  15.4 us (4%)
  other arithmetic  14.9 us (4%)
  between operations  14.2 us (4%)
    all_to_all x1, waiting for transfers between devices, body(): lax.all_to_all(grad_send, 'fsdp', split_axis=0, concat_axis=0, tiled=True)  133 us
    all_to_all x1, waiting for transfers between devices, body(): lax.all_to_all(partial_value, 'fsdp', split_axis=0, concat_axis=0, tiled=...  73 us
    reduce_scatter x1, waiting for transfers between devices, body(): lax.psum_scatter(lax.dot_general(columns, grad_flat, (((0,), (0,)), ((),...  55 us
    all_gather x1, waiting for transfers between devices, body(): lax.all_gather(query_weight, 'fsdp', axis=0, tiled=True)  51 us
  transfers between devices with their start and end apart: 5, of which 5 were waited for; matrix products, arithmetic and copies ran while one was open for 6% of the time, Pallas kernels for 0%

commit v1 on v0

v1 whole, which is shorter than its diff:
```python
import jax
import jax.numpy as jnp
from jax import lax
from jax.sharding import Mesh, PartitionSpec as P

INNER = 4


def body(tokens, owner, row_pick, query_weight, sub_keys, values, cotangent):
    tok_rows = tokens.shape[0]
    heads = owner.shape[1]
    width = tokens.shape[1]
    block_rows = values.shape[0]
    key_width = sub_keys.shape[2]
    far = lax.axis_size("far")
    near = lax.axis_size("near")
    copies = lax.axis_size("dp")
    groups = far * near
    layer = near * copies
    part = width // layer
    capacity = max(2, 3 * tok_rows * heads // (2 * groups))
    requests = tok_rows * heads
    f32, bf16 = jnp.float32, jnp.bfloat16
    y = lax.axis_index("dp")

    cot = cotangent.reshape(tok_rows, layer, part).transpose(1, 0, 2)
    cot = lax.all_to_all(cot, ("near", "dp"), split_axis=0, concat_axis=0, tiled=True)
    cot = lax.all_gather(cot, "far", axis=0, tiled=False)

    vals = values.reshape(block_rows, near, copies, part)
    vals = lax.dynamic_index_in_dim(vals, y, axis=2, keepdims=False).transpose(1, 0, 2)
    vals = lax.all_to_all(vals, "near", split_axis=0, concat_axis=0, tiled=True)

    own = query_weight.shape[0] // copies
    mine = lax.dynamic_slice_in_dim(query_weight, y * own, own, axis=0)
    qw = lax.all_gather(mine, ("far", "near", "dp"), axis=0, tiled=True)
    query = jnp.dot(tokens, qw, preferred_element_type=f32).astype(bf16)
    query = query.reshape(tok_rows, heads, key_width)
    full = jnp.einsum("thk,hrk->thr", query, sub_keys, preferred_element_type=f32)
    match = row_pick[:, :, :, None] == jnp.arange(block_rows, dtype=jnp.int32)[None, None, None, :]
    picked = jnp.sum(jnp.where(match, full[:, :, None, :], 0.0), axis=3)
    score = picked * (1.0 / key_width**0.5)
    top = jnp.max(score, axis=2, keepdims=True)
    expo = jnp.exp(score - top)
    weight = (expo / jnp.sum(expo, axis=2, keepdims=True)).astype(bf16)
    table = jnp.sum(jnp.where(match, weight.astype(f32)[:, :, :, None], 0.0), axis=2)
    table = table.astype(bf16).reshape(requests, block_rows)

    ids = jnp.arange(groups, dtype=jnp.int32)
    hits = owner[:, :, None] == ids[None, None, :]
    named = jnp.any(hits, axis=1)
    row = jnp.arange(tok_rows, dtype=jnp.int32)
    before = (row[:, None] > row[None, :]).astype(bf16)
    rank = jnp.dot(before, named.astype(bf16), preferred_element_type=f32).astype(jnp.int32)
    places = jnp.arange(capacity, dtype=jnp.int32)
    own_slot = hits & (rank[:, None, :] < capacity)
    slot = jnp.sum(jnp.where(own_slot, ids * capacity + rank[:, None, :], 0), axis=2).reshape(-1)
    dispatch = (
        jnp.arange(groups * capacity, dtype=jnp.int32)[:, None] == slot[None, :]
    ).astype(bf16)
    send = jnp.dot(dispatch, table, preferred_element_type=f32).astype(bf16)
    send = send.reshape(groups, capacity, block_rows)
    held = named[:, :, None] & (rank[:, :, None] == places)
    who = jnp.sum(jnp.where(held, row[:, None, None] + 1, 0), axis=0) - 1
    who = jnp.pad(who, ((0, 0), (0, block_rows - capacity)), constant_values=-1)
    send = jnp.concatenate([send, who.astype(bf16)[:, None, :]], axis=1)
    send = send.reshape(far, near, capacity + 1, block_rows)
    got = lax.all_to_all(send, "far", split_axis=0, concat_axis=0, tiled=True)
    got = lax.all_gather(got, ("near", "dp"), axis=0, tiled=False)
    got = got.transpose(1, 0, 2, 3, 4).reshape(far * layer, near, capacity + 1, block_rows)
    slots = got[:, :, :capacity, :]
    who = got[:, :, capacity, :capacity]
    pick = (who[:, None, :, :] == row.astype(bf16)[None, :, None, None]).astype(bf16)
    pick = pick.reshape(far * layer, tok_rows, near * capacity)
    cot = cot.reshape(far * layer, tok_rows, part)

    reads = jnp.einsum("dlcr,lrw->dlcw", slots, vals, preferred_element_type=f32).astype(bf16)
    reads = reads.reshape(far * layer, near * capacity, part)
    partial = jnp.einsum("dts,dsw->dtw", pick, reads, preferred_element_type=f32).astype(bf16)
    partial = partial.reshape(far, layer, tok_rows, part)
    total = lax.psum_scatter(partial, "far", scatter_dimension=0, tiled=False)
    total = lax.all_to_all(total, ("near", "dp"), split_axis=0, concat_axis=0, tiled=True)
    memory_out = total.transpose(1, 0, 2).reshape(tok_rows, width)

    terms = jnp.einsum("dts,dtw->dsw", pick, cot, preferred_element_type=f32).astype(bf16)
    terms = terms.reshape(far * layer, near, capacity, part)
    grad = jnp.einsum("dlcr,dlcw->lrw", slots, terms, preferred_element_type=f32).astype(bf16)
    grad = grad.reshape(layer, block_rows // copies, part)
    grad = lax.all_to_all(grad, ("near", "dp"), split_axis=0, concat_axis=0, tiled=True)
    grad_values = grad.transpose(1, 0, 2).reshape(block_rows // copies, width)
    return memory_out, grad_values


def solution(mesh):
    fsdp, dp = mesh.shape["fsdp"], mesh.shape["dp"]
    fine = Mesh(mesh.devices.reshape(fsdp // INNER, INNER, dp), ("far", "near", "dp"))
    rows, held = ("far", "near", "dp"), ("far", "near")
    placed = (
        P(rows, None),
        P(rows, None),
        P(rows, None, None),
        P(held, None),
        P(),
        P(held, None),
        P(rows, None),
    )
    return jax.shard_map(
        body,
        mesh=fine,
        in_specs=placed,
        out_specs=(P(rows, None), P(rows, None)),
        check_vma=False,
    )
```

time: 392 us -> 335 us (0.85)
  the two profiles are of different devices: /device:TPU:11 before, /device:TPU:0 now
where the time goes in v1:
time: 335 us; the launch traced here: 334 us
  waiting for transfers between devices  205 us (61%)
  blocking collectives  54.8 us (16%)
  local copies, waits for them, and re-layouts  20.3 us (6%)
  matrix products  18.5 us (6%)
  other arithmetic  14.1 us (4%)
  between operations  14 us (4%)
  starting transfers between devices  7.52 us (2%)
    all_gather x1, waiting for transfers between devices, body(): cot = lax.all_gather(cot, 'far', axis=0, tiled=False)  65.2 us
    all_gather x1, waiting for transfers between devices, body(): qw = lax.all_gather(mine, ('far', 'near', 'dp'), axis=0, tiled=True)  63.7 us
    reduce_scatter x1, waiting for transfers between devices, body(): total = lax.psum_scatter(partial, 'far', scatter_dimension=0, tiled=False)  53.3 us
    all_to_all x1, blocking collectives, body(): lax.all_to_all(cot, ('near', 'dp'), split_axis=0, concat_axis=0, tiled=True)  21.3 us
    all_to_all x1, blocking collectives, body(): lax.all_to_all(grad, ('near', 'dp'), split_axis=0, concat_axis=0, tiled=T...  17.9 us
    all_to_all x1, blocking collectives, body(): got = lax.all_to_all(send, 'far', split_axis=0, concat_axis=0, tiled=True)  15.6 us
    all_to_all x1, waiting for transfers between devices, body(): lax.all_to_all(total, ('near', 'dp'), split_axis=0, concat_axis=0, tiled=...  13.4 us
  transfers between devices with their start and end apart: 6, of which 6 were waited for; matrix products, arithmetic and copies ran while one was open for 9% of the time, Pallas kernels for 0%

profile of v1, /device:TPU:0, one launch (start us, length us, event | category | flops | bytes accessed | tf_op | source)
XLA Modules:
  0.0 334.4 jit_solution(13223066105212573920)
XLA Ops:
  7.2 1.7 constant_dynamic-slice_fusion.1
  12.2 63.7 %all-gather.6.cloned.1.call-done = bf16[4096,512]{1,0:T(8,128)(2,1)} async-done(((bf16[128,512]{1,0:T(8,128)(2,1)}), bf16[4096,512]{1,0:T(8,128)(2,1)}) %all-gather.6.cloned.1.call-update) | async-done | bytes 4194320 | tf_op jit(solution)/shard_map/all_gather | solution.py:36
  75.9 3.5 %convolution_convert_fusion = bf16[512,128]{1,0:T(8,128)(2,1)S(1)} fusion(bf16[4096,512]{1,0:T(8,128)(2,1)} %all-gather.6.cloned.1.call-done, bf16[128,4096]{1,0:T(8,128)(2,1)S(1)} %copy-done), kind=kOutput, calls=%fused_computation.21 | convolution fusion | flops 536936448 | bytes 5373952 | tf_op jit(solution)/shard_map/dot_general | solution.py:37
  80.1 5.3 %select_reduce_fusion.1 = f32[128,4,32]{2,1,0:T(4,128)S(1)} fusion(f32[128,4,256]{2,1,0:T(4,128)S(1)} %copy.78, s32[128,4,32]{2,1,0:T(4,128)S(1)} %copy.76), kind=kLoop, calls=%fused_computation.3 | loop fusion | flops 12566528 | bytes 655360 | tf_op jit(solution)/shard_map/reduce_sum | solution.py:41
  85.7 6.6 %select_reduce_fusion = bf16[128,4,256]{2,1,0:T(4,128)(2,1)S(1)} fusion(f32[128,4,32]{2,1,0:T(4,128)S(1)} %copy.80, s32[128,4,32]{2,1,0:T(4,128)S(1)} %copy.76), kind=kLoop, calls=%fused_computation.2 | loop fusion | flops 12451840 | bytes 393216 | tf_op jit(solution)/shard_map/reduce_sum | solution.py:46
  93.3 15.6 %all_to_all.25 = bf16[4,4,49,256]{3,1,2,0:T(4,128)(2,1)} all-to-all(bf16[4,4,49,256]{3,1,2,0:T(4,128)(2,1)S(1)} %pad_maximum_fusion), channel_id=1, replica_groups=mesh['far'=4,'near'=4,'dp'=2] {'far'}, dimensions={0} | all-to-all | bytes 802816 | tf_op jit(solution)/shard_map/all_to_all | solution.py:68
  109.7 21.3 %all_to_all.26 = bf16[8,128,512]{1,2,0:T(8,128)(2,1)S(1)} all-to-all(bf16[8,128,512]{1,2,0:T(8,128)(2,1)S(1)} %bitcast.55), channel_id=1, replica_groups=mesh['far'=4,'near'=4,'dp'=2] {'near','dp'}, dimensions={0} | all-to-all | bytes 2097152 | tf_op jit(solution)/shard_map/all_to_all | solution.py:27
  132.3 3.5 %reshape.87 = bf16[256,4,2,512]{3,2,1,0:T(2,128)(2,1)S(1)} reshape(bf16[256,4096]{1,0:T(8,128)(2,1)} %param.12) | data formatting | bytes 4194304 | tf_op jit(solution)/shard_map/reshape | solution.py:30
  135.7 2.2 constant_dynamic-slice_fusion
  137.9 1.5 copy.103
  139.5 3.5 %all-to-all-start.1 = ((bf16[4,256,512]{2,1,0:T(8,128)(2,1)}), bf16[4,256,512]{2,1,0:T(8,128)(2,1)S(1)}, u32[]{:S(2)}, u32[]{:S(2)}) async-start(bf16[4,256,512]{2,1,0:T(8,128)(2,1)} %bitcast.49), calls=%async_computation.1 | async-start | bytes 2097152 | tf_op jit(solution)/shard_map/all_to_all | solution.py:32
  143.2 3.7 %all-gather.8.cloned.1.call-done = bf16[32,4,49,256]{3,1,2,0:T(4,128)(2,1)} async-done(((bf16[4,4,49,256]{3,1,2,0:T(4,128)(2,1)}), bf16[32,4,49,256]{3,1,2,0:T(4,128)(2,1)}) %all-gather.8.cloned.1.call-update) | async-done | bytes 3211280 | tf_op jit(solution)/shard_map/all_gather | solution.py:69
  146.9 2.5 copy.83
  149.4 1.9 copy-done.1
  151.5 5.9 %all-to-all-done.1 = bf16[4,256,512]{2,1,0:T(8,128)(2,1)S(1)} async-done(((bf16[4,256,512]{2,1,0:T(8,128)(2,1)}), bf16[4,256,512]{2,1,0:T(8,128)(2,1)S(1)}, u32[]{:S(2)}, u32[]{:S(2)}) %all-to-all-start.1) | async-done | bytes 1048608 | tf_op jit(solution)/shard_map/all_to_all | solution.py:32
  157.4 4.0 %convert_bitcast_fusion = bf16[32,4,48,512]{3,2,0,1:T(8,128)(2,1)S(1)} fusion(bf16[32,4,49,256]{3,2,0,1:T(8,128)(2,1)} %bitcast.57, bf16[4,256,512]{2,1,0:T(8,128)(2,1)S(1)} %all-to-all-done.1), kind=kOutput, calls=%fused_computation.7 | convolution fusion | flops 1613758464 | bytes 10485760 | tf_op jit(solution)/shard_map/dlcr,lrw->dlcw/dot_general | solution.py:77
  162.0 3.9 %fusion.13 = bf16[32,128,512]{2,1,0:T(8,128)(2,1)} fusion(bf16[32,192,512]{2,1,0:T(8,128)(2,1)S(1)} %bitcast.50, bf16[128]{0:T(256)(128)(2,1)S(1)} %iota_convert_fusion, bf16[32,192]{1,0:T(8,128)(2,1)S(1)} %eq.83), kind=kOutput, calls=%fused_computation.15 | convolution fusion | flops 808189952 | bytes 10498304 | tf_op jit(solution)/shard_map/dts,dsw->dtw/dot_general | solution.py:79
  166.0 65.2 %all-gather.10.cloned.1.call-done = bf16[32,128,512]{2,1,0:T(8,128)(2,1)} async-done(((bf16[8,128,512]{2,1,0:T(8,128)(2,1)}), bf16[32,128,512]{2,1,0:T(8,128)(2,1)}) %all-gather.10.cloned.1.call-update) | async-done | bytes 4194320 | tf_op jit(solution)/shard_map/all_gather | solution.py:28
  231.2 4.4 %fusion.8 = bf16[32,192,512]{2,1,0:T(8,128)(2,1)S(1)} fusion(bf16[32,128,512]{2,1,0:T(8,128)(2,1)} %all-gather.10.cloned.1.call-done, bf16[128]{0:T(256)(128)(2,1)S(1)} %iota_convert_fusion, bf16[32,192]{1,0:T(8,128)(2,1)S(1)} %eq.83), kind=kOutput, calls=%fused_computation.12 | convolution fusion | flops 809238528 | bytes 10498304 | tf_op jit(solution)/shard_map/dts,dtw->dsw/dot_general | solution.py:85
  235.6 1.8 bitcast_convert_fusion
  237.5 17.9 %all_to_all.27 = bf16[8,128,512]{2,1,0:T(8,128)(2,1)S(1)} all-to-all(bf16[8,128,512]{2,1,0:T(8,128)(2,1)S(1)} %bitcast.63), channel_id=1, replica_groups=mesh['far'=4,'near'=4,'dp'=2] {'near','dp'}, dimensions={0} | all-to-all | bytes 2097152 | tf_op jit(solution)/shard_map/all_to_all | solution.py:89
  255.3 53.3 %reduce-scatter.2.cloned.1.call-done = bf16[1,8,128,512]{3,2,1,0:T(8,128)(2,1)} async-done(((bf16[4,8,128,512]{3,2,1,0:T(8,128)(2,1)}), bf16[1,8,128,512]{3,2,1,0:T(8,128)(2,1)}) %reduce-scatter.2.cloned.1.call-update) | async-done | bytes 1048592 | tf_op jit(solution)/shard_map/reduce_scatter | solution.py:81
  308.6 3.7 %all-to-all-start.2 = ((bf16[8,128,512]{2,1,0:T(8,128)(2,1)}), bf16[8,128,512]{2,1,0:T(8,128)(2,1)S(1)}, u32[]{:S(2)}, u32[]{:S(2)}) async-start(bf16[8,128,512]{2,1,0:T(8,128)(2,1)} %bitcast.60), calls=%async_computation.3 | async-start | bytes 2097152 | tf_op jit(solution)/shard_map/all_to_all | solution.py:82
  313.4 13.4 %all-to-all-done.2 = bf16[8,128,512]{2,1,0:T(8,128)(2,1)S(1)} async-done(((bf16[8,128,512]{2,1,0:T(8,128)(2,1)}), bf16[8,128,512]{2,1,0:T(8,128)(2,1)S(1)}, u32[]{:S(2)}, u32[]{:S(2)}) %all-to-all-start.2) | async-done | bytes 1048608 | tf_op jit(solution)/shard_map/all_to_all | solution.py:82
  (48 shorter events, 10.4 us)
Async XLA Ops:
  7.2 68.8 %copy-start = (bf16[128,4096]{1,0:T(8,128)(2,1)S(1)}, bf16[128,4096]{1,0:T(8,128)(2,1)}, u32[]{:S(2)}) copy-start(bf16[128,4096]{1,0:T(8,128)(2,1)} %param.7) | copy-start | bytes 3145732
  7.2 72.2 %copy-start.4 = (bf16[4,256,128]{2,1,0:T(8,128)(2,1)S(1)}, bf16[4,256,128]{2,1,0:T(8,128)(2,1)}, u32[]{:S(2)}) copy-start(bf16[4,256,128]{2,1,0:T(8,128)(2,1)} %param.11) | copy-start | bytes 786436
  7.2 68.7 %all-gather.6.cloned.1.call-start = ((), (), s32[]{:S(2)}) async-start(), calls=%async_computation.6 | async-start | bytes 4325376 | tf_op jit(solution)/shard_map/all_gather | solution.py:36
  8.9 138.0 %all-gather.8.cloned.1.call-start = ((), (), s32[]{:S(2)}) async-start(), calls=%async_computation.8 | async-start | bytes 3612672 | tf_op jit(solution)/shard_map/all_gather | solution.py:69
  79.7 29.3 %copy-start.3 = (bf16[128,4096]{1,0:T(8,128)(2,1)S(1)}, bf16[128,4096]{1,0:T(8,128)(2,1)}, u32[]{:S(2)}) copy-start(bf16[128,4096]{1,0:T(8,128)(2,1)} %param.13) | copy-start | bytes 3145732
  108.9 122.2 %all-gather.10.cloned.1.call-start = ((), (), s32[]{:S(2)}) async-start(), calls=%async_computation.9 | async-start | bytes 5242880 | tf_op jit(solution)/shard_map/all_gather | solution.py:28
  139.5 17.9 %all-to-all-start.1 = ((bf16[4,256,512]{2,1,0:T(8,128)(2,1)}), bf16[4,256,512]{2,1,0:T(8,128)(2,1)S(1)}, u32[]{:S(2)}, u32[]{:S(2)}) async-start(bf16[4,256,512]{2,1,0:T(8,128)(2,1)} %bitcast.49), calls=%async_computation.1 | async-start | bytes 2097152 | tf_op jit(solution)/shard_map/all_to_all | solution.py:32
  143.0 165.7 %reduce-scatter.2.cloned.1.call-start = ((), (), s32[]{:S(2)}) async-start(), calls=%async_computation.7 | async-start | bytes 5242880 | tf_op jit(solution)/shard_map/reduce_scatter | solution.py:81
  149.4 1.9 copy-start.1
  231.2 4.5 %copy-start.2 = (bf16[8,4,4,49,256]{4,3,0,1,2:T(8,128)(2,1)S(1)}, bf16[8,4,4,49,256]{4,3,0,1,2:T(8,128)(2,1)}, u32[]{:S(2)}) copy-start(bf16[8,4,4,49,256]{4,3,0,1,2:T(8,128)(2,1)} %copy-done.1) | copy-start | bytes 9633796
  308.6 18.2 %all-to-all-start.2 = ((bf16[8,128,512]{2,1,0:T(8,128)(2,1)}), bf16[8,128,512]{2,1,0:T(8,128)(2,1)S(1)}, u32[]{:S(2)}, u32[]{:S(2)}) async-start(bf16[8,128,512]{2,1,0:T(8,128)(2,1)} %bitcast.60), calls=%async_computation.3 | async-start | bytes 2097152 | tf_op jit(solution)/shard_map/all_to_all | solution.py:82
Sparse Core Ops, SparseCore 0:
  11.5 64.4 all-gather.5
  109.0 37.7 all-gather.7
  149.0 82.0 all-gather.9
  233.3 75.2 reduce-scatter.1

commit v2 on v1

--- a/solution.py
+++ b/solution.py
@@ -1,9 +1,182 @@
+import functools
 import jax
 import jax.numpy as jnp
 from jax import lax
+from jax.experimental import pallas as pl
+from jax.experimental.pallas import tpu as pltpu
 from jax.sharding import Mesh, PartitionSpec as P
 
 INNER = 4
+MESH = pl.DeviceIdType.MESH
+AXES = ("far", "high", "low", "dp")
+ORDERS = (("far", "dp", "high", "low"), ("far", "high", "dp", "low"))
+
+
+def place():
+    near = lax.axis_index("near")
+    return (lax.axis_index("far"), near // 2, near % 2, lax.axis_index("dp"))
+
+
+def moved(me, sizes, off):
+    return tuple(lax.rem(m + o, n) if o else m for m, o, n in zip(me, off, sizes))
+
+
+def device(spot):
+    return {"far": spot[0], "near": spot[1] * 2 + spot[2], "dp": spot[3]}
+
+
+def tree(order, sizes):
+    nodes = [((0, 0, 0, 0), -1, [])]
+    for off, stage, copies in nodes:
+        for k in range(stage + 1, len(order)):
+            axis = AXES.index(order[k])
+            for r in range(1, sizes[axis]):
+                child = list(off)
+                child[axis] = (child[axis] - r) % sizes[axis]
+                copies.append((axis, r, len(nodes)))
+                nodes.append((tuple(child), k, []))
+    return nodes
+
+
+def greet(peers):
+    barrier = pltpu.get_barrier_semaphore()
+    for spot in peers:
+        pl.semaphore_signal(barrier, inc=1, device_id=device(spot), device_id_type=MESH)
+    pl.semaphore_wait(barrier, len(peers))
+
+
+def steps(sizes):
+    found = []
+    for axis, n in enumerate(sizes):
+        for r in range(1, n):
+            found.append(tuple(r if a == axis else 0 for a in range(4)))
+    return found
+
+
+def spread(me, sizes, plans, own, slot, started, send_sem, recv_sem):
+    pending = {}
+    longest = max(len(nodes) for nodes in plans)
+    for number in range(longest):
+        for item, nodes in enumerate(plans):
+            if number >= len(nodes):
+                continue
+            off, stage, copies = nodes[number]
+            if number:
+                pending[item, number].wait_recv()
+            here = moved(me, sizes, off)
+            for axis, r, child in copies:
+                step = tuple(r if a == axis else 0 for a in range(4))
+                peer = moved(me, sizes, step)
+                copy = pltpu.make_async_remote_copy(
+                    src_ref=slot(item, here) if number else own(item, axis, peer),
+                    dst_ref=slot(item, here),
+                    send_sem=send_sem.at[item, child],
+                    recv_sem=recv_sem.at[item, child],
+                    device_id=device(peer),
+                    device_id_type=MESH,
+                )
+                copy.start()
+                pending[item, child] = copy
+                started.append(copy)
+
+
+def gather_kernel(sizes, qw_ref, val_ref, out_ref, vals_ref, send_sem, recv_sem, vsend, vrecv):
+    me = place()
+    half = qw_ref.shape[0] // 2
+    part = vals_ref.shape[2]
+    corner = (0, 1, 1, 0)
+    greet([moved(me, sizes, s) for s in steps(sizes) + [corner]])
+    for item in range(2):
+        out_ref[me[0], me[1], me[2], me[3], item] = qw_ref[pl.ds(item * half, half), :]
+    started = []
+
+    def own(item, axis, peer):
+        return qw_ref.at[pl.ds(item * half, half), :]
+
+    def slot(item, spot):
+        return out_ref.at[spot[0], spot[1], spot[2], spot[3], item]
+
+    plans = [tree(order, sizes) for order in ORDERS]
+    spread(me, sizes, plans, own, slot, started, send_sem, recv_sem)
+    pushes = []
+    for number, step in enumerate(((0, 1, 0, 0), (0, 0, 1, 0), corner)):
+        peer = moved(me, sizes, step)
+        first = ((peer[1] * 2 + peer[2]) * sizes[3] + peer[3]) * part
+        copy = pltpu.make_async_remote_copy(
+            src_ref=val_ref.at[:, pl.ds(pl.multiple_of(first, part), part)],
+            dst_ref=vals_ref.at[me[1] * 2 + me[2]],
+            send_sem=vsend.at[number],
+            recv_sem=vrecv.at[number],
+            device_id=device(peer),
+            device_id_type=MESH,
+        )
+        copy.start()
+        pushes.append(copy)
+    first = ((me[1] * 2 + me[2]) * sizes[3] + me[3]) * part
+    vals_ref[me[1] * 2 + me[2]] = val_ref[:, pl.ds(pl.multiple_of(first, part), part)]
+    for copy in started:
+        copy.wait_send()
+    for copy in pushes:
+        copy.wait()
+
+
+def table_kernel(sizes, send_ref, out_ref, send_sem, recv_sem):
+    me = place()
+    half = send_ref.shape[2] // 2
+    greet([moved(me, sizes, s) for s in steps(sizes)])
+    out_ref[me[0], me[1], me[2], me[3]] = send_ref[me[0]]
+    started = []
+
+    def own(item, axis, peer):
+        return send_ref.at[peer[0], :, pl.ds(item * half, half)]
+
+    def slot(item, spot):
+        return out_ref.at[spot[0], spot[1], spot[2], spot[3], :, pl.ds(item * half, half)]
+
+    plans = [tree(order, sizes) for order in ORDERS]
+    spread(me, sizes, plans, own, slot, started, send_sem, recv_sem)
+    for copy in started:
+        copy.wait_send()
+
+
+VMEM = pl.BlockSpec(memory_space=pltpu.VMEM)
+
+
+def gather(sizes, mine, values, near, part):
+    count = sizes[0] * sizes[1] * sizes[2] * sizes[3]
+    return pl.pallas_call(
+        functools.partial(gather_kernel, sizes),
+        out_shape=(
+            jax.ShapeDtypeStruct(sizes + (2, mine.shape[0] // 2, mine.shape[1]), mine.dtype),
+            jax.ShapeDtypeStruct((near, values.shape[0], part), values.dtype),
+        ),
+        in_specs=[VMEM] * 2,
+        out_specs=(VMEM, VMEM),
+        scratch_shapes=[
+            pltpu.SemaphoreType.DMA((2, count)),
+            pltpu.SemaphoreType.DMA((2, count)),
+            pltpu.SemaphoreType.DMA((3,)),
+            pltpu.SemaphoreType.DMA((3,)),
+        ],
+        compiler_params=pltpu.CompilerParams(collective_id=0, has_side_effects=True),
+        name="gather_rows",
+    )(mine, values)
+
+
+def exchange(sizes, send):
+    count = sizes[0] * sizes[1] * sizes[2] * sizes[3]
+    return pl.pallas_call(
+        functools.partial(table_kernel, sizes),
+        out_shape=jax.ShapeDtypeStruct(sizes + send.shape[1:], send.dtype),
+        in_specs=[VMEM],
+        out_specs=VMEM,
+        scratch_shapes=[
+            pltpu.SemaphoreType.DMA((2, count)),
+            pltpu.SemaphoreType.DMA((2, count)),
+        ],
+        compiler_params=pltpu.CompilerParams(collective_id=1, has_side_effects=True),
+        name="exchange_tables",
+    )(send)
 
 
 def body(tokens, owner, row_pick, query_weight, sub_keys, values, cotangent):
@@ -27,13 +200,11 @@
     cot = lax.all_to_all(cot, ("near", "dp"), split_axis=0, concat_axis=0, tiled=True)
     cot = lax.all_gather(cot, "far", axis=0, tiled=False)
 
-    vals = values.reshape(block_rows, near, copies, part)
-    vals = lax.dynamic_index_in_dim(vals, y, axis=2, keepdims=False).transpose(1, 0, 2)
-    vals = lax.all_to_all(vals, "near", split_axis=0, concat_axis=0, tiled=True)
-
     own = query_weight.shape[0] // copies
     mine = lax.dynamic_slice_in_dim(query_weight, y * own, own, axis=0)
-    qw = lax.all_gather(mine, ("far", "near", "dp"), axis=0, tiled=True)
+    sizes = (far, 2, near // 2, copies)
+    qw, vals = gather(sizes, mine, values, near, part)
+    qw = qw.reshape(width, -1)
     query = jnp.dot(tokens, qw, preferred_element_type=f32).astype(bf16)
     query = query.reshape(tok_rows, heads, key_width)
     full = jnp.einsum("thk,hrk->thr", query, sub_keys, preferred_element_type=f32)
@@ -62,14 +233,13 @@
     send = send.reshape(groups, capacity, block_rows)
     held = named[:, :, None] & (rank[:, :, None] == places)
     who = jnp.sum(jnp.where(held, row[:, None, None] + 1, 0), axis=0) - 1
-    who = jnp.pad(who, ((0, 0), (0, block_rows - capacity)), constant_values=-1)
-    send = jnp.concatenate([send, who.astype(bf16)[:, None, :]], axis=1)
-    send = send.reshape(far, near, capacity + 1, block_rows)
-    got = lax.all_to_all(send, "far", split_axis=0, concat_axis=0, tiled=True)
-    got = lax.all_gather(got, ("near", "dp"), axis=0, tiled=False)
-    got = got.transpose(1, 0, 2, 3, 4).reshape(far * layer, near, capacity + 1, block_rows)
-    slots = got[:, :, :capacity, :]
-    who = got[:, :, capacity, :capacity]
+    spare = 16 * -(-near // 16)
+    who = who.astype(bf16).reshape(far, near, capacity)
+    who = jnp.pad(who, ((0, 0), (0, spare - near), (0, block_rows - capacity)))
+    send = jnp.concatenate([send.reshape(far, near * capacity, block_rows), who], axis=1)
+    got = exchange(sizes, send).reshape(far * layer, near * capacity + spare, block_rows)
+    slots = got[:, : near * capacity].reshape(far * layer, near, capacity, block_rows)
+    who = got[:, near * capacity : near * capacity + near, :capacity]
     pick = (who[:, None, :, :] == row.astype(bf16)[None, :, None, None]).astype(bf16)
     pick = pick.reshape(far * layer, tok_rows, near * capacity)
     cot = cot.reshape(far * layer, tok_rows, part)

time: 335 us -> 256 us (0.76)
  waiting for transfers between devices: 205 us -> 68.6 us
  Pallas kernels: 0 us -> 88.1 us
  blocking collectives: 54.8 us -> 36.4 us
  local copies, waits for them, and re-layouts: 20.3 us -> 12.5 us
  starting transfers between devices: 7.52 us -> 3.71 us
    pallas_call x0 -> x2, Pallas kernels: none -> 88.1 us  [the longest x1 51.5 us: gather(): pl.pallas_call(functools.partial(gather_kernel, sizes), out_shape=(jax.Sh...]
    all_gather x2 -> x0, waiting for transfers between devices: 67.4 us -> none  [the longest x1 63.7 us: body(): qw = lax.all_gather(mine, ('far', 'near', 'dp'), axis=0, tiled=True)]
    all_gather x1, waiting for transfers between devices: 65.2 us -> 0.02 us  [body(): cot = lax.all_gather(cot, 'far', axis=0, tiled=False)]
    all_to_all x1 -> x0, blocking collectives: 15.6 us -> none  [body(): got = lax.all_to_all(send, 'far', split_axis=0, concat_axis=0, tiled=True)]
    all_to_all x1 -> x0, waiting for transfers between devices: 5.91 us -> none  [body(): vals = lax.all_to_all(vals, 'near', split_axis=0, concat_axis=0, tiled=True)]
    slice x2, local copies, waits for them, and re-layouts: 0.08 us -> 4.84 us  [the longest x1 3.98 us: body(): got[:, :near * capacity].reshape(far * layer, near, capacity, block_rows)]
    all_to_all x1 -> x0, starting transfers between devices: 3.52 us -> none  [body(): vals = lax.all_to_all(vals, 'near', split_axis=0, concat_axis=0, tiled=True)]
    reshape x1 -> x0, local copies, waits for them, and re-layouts: 3.46 us -> none  [body(): vals = values.reshape(block_rows, near, copies, part)]
  transfers between devices with their start and end apart: 6 -> 3, of which waited for: 6 -> 2; matrix products, arithmetic and copies ran while one was open for 9% -> 16% of each run, Pallas kernels for 0% -> 35%
where the time goes in v2:
time: 256 us; the launch traced here: 255 us
  Pallas kernels  88.1 us (34%)
  waiting for transfers between devices  68.6 us (27%)
  blocking collectives  36.4 us (14%)
  matrix products  18.2 us (7%)
  between operations  14.4 us (6%)
  other arithmetic  13.4 us (5%)
  local copies, waits for them, and re-layouts  12.5 us (5%)
  starting transfers between devices  3.71 us (1%)
    reduce_scatter x1, waiting for transfers between devices, body(): total = lax.psum_scatter(partial, 'far', scatter_dimension=0, tiled=False)  55.1 us
    pallas_call x1, Pallas kernels, gather(): pl.pallas_call(functools.partial(gather_kernel, sizes), out_shape=(jax.Sh...  51.5 us
    pallas_call x1, Pallas kernels, exchange(): pl.pallas_call(functools.partial(table_kernel, sizes), out_shape=jax.Shap...  36.6 us
    all_to_all x1, blocking collectives, body(): lax.all_to_all(cot, ('near', 'dp'), split_axis=0, concat_axis=0, tiled=True)  19.4 us
    all_to_all x1, blocking collectives, body(): lax.all_to_all(grad, ('near', 'dp'), split_axis=0, concat_axis=0, tiled=T...  17 us
    all_to_all x1, waiting for transfers between devices, body(): lax.all_to_all(total, ('near', 'dp'), split_axis=0, concat_axis=0, tiled=...  13.4 us
    reduce_sum x1, other arithmetic, body(): jnp.sum(jnp.where(match, weight.astype(f32)[:, :, :, None], 0.0), axis=2)  6.6 us
    reduce_sum x1, other arithmetic, body(): picked = jnp.sum(jnp.where(match, full[:, :, None, :], 0.0), axis=3)  5.5 us
  transfers between devices with their start and end apart: 3, of which 2 were waited for; matrix products, arithmetic and copies ran while one was open for 16% of the time, Pallas kernels for 35%

profile of v2, /device:TPU:0, one launch (start us, length us, event | category | flops | bytes accessed | tf_op | source)
XLA Modules:
  0.0 255.2 jit_solution(16118162634257649085)
XLA Ops:
  7.3 1.7 copy.70
  9.0 19.4 %all_to_all.15 = bf16[8,128,512]{1,2,0:T(8,128)(2,1)S(1)} all-to-all(bf16[8,128,512]{1,2,0:T(8,128)(2,1)S(1)} %bitcast.50), channel_id=1, replica_groups=mesh['far'=4,'near'=4,'dp'=2] {'near','dp'}, dimensions={0} | all-to-all | bytes 2097152 | tf_op jit(solution)/shard_map/all_to_all | solution.py:200
  28.4 1.3 copy.71
  30.4 0.7 constant_dynamic-slice_fusion.qw_ref
  31.1 51.5 %gather_rows.1 = (bf16[4,2,2,2,2,64,512]{6,5,4,3,2,1,0:T(8,128)(2,1)}, bf16[4,256,512]{2,1,0:T(8,128)(2,1)}) custom-call(bf16[128,512]{1,0:T(8,128)(2,1)} %constant_dynamic-slice_fusion.qw_ref, bf16[256,4096]{1,0:T(8,128)(2,1)} %val_ref.1), custom_call_target="tpu_custom_call" | custom-call | tf_op jit(solution)/shard_map/gather_rows/pallas_call | solution.py:147
  82.6 3.5 %convolution_convert_fusion = bf16[512,128]{1,0:T(8,128)(2,1)S(1)} fusion(bf16[4096,512]{1,0:T(8,128)(2,1)} %bitcast.60, bf16[128,4096]{1,0:T(8,128)(2,1)S(1)} %copy-done), kind=kOutput, calls=%fused_computation.18 | convolution fusion | flops 536936448 | bytes 5373952 | tf_op jit(solution)/shard_map/dot_general | solution.py:208
  86.7 5.5 %select_reduce_fusion.1 = f32[128,4,32]{2,1,0:T(4,128)S(1)} fusion(f32[128,4,256]{2,1,0:T(4,128)S(1)} %copy.64, s32[128,4,32]{2,1,0:T(4,128)S(1)} %copy.62), kind=kLoop, calls=%fused_computation.3 | loop fusion | flops 12566528 | bytes 655360 | tf_op jit(solution)/shard_map/reduce_sum | solution.py:212
  92.5 6.6 %select_reduce_fusion = bf16[128,4,256]{2,1,0:T(4,128)(2,1)S(1)} fusion(f32[128,4,32]{2,1,0:T(4,128)S(1)} %copy.66, s32[128,4,32]{2,1,0:T(4,128)S(1)} %copy.62), kind=kLoop, calls=%fused_computation.2 | loop fusion | flops 12451840 | bytes 393216 | tf_op jit(solution)/shard_map/reduce_sum | solution.py:217
  99.6 0.4 fusion.14
  100.0 0.8 fusion.27.send_ref
  100.8 36.6 %exchange_tables.1 = bf16[4,2,2,2,208,256]{5,4,3,2,1,0:T(8,128)(2,1)} custom-call(bf16[4,208,256]{2,1,0:T(8,128)(2,1)} %fusion.27.send_ref), custom_call_target="tpu_custom_call" | custom-call | tf_op jit(solution)/shard_map/exchange_tables/pallas_call | solution.py:168
  137.4 0.9 slice.8
  138.3 4.0 %slice.9 = bf16[32,192,256]{2,1,0:T(8,128)(2,1)} slice(bf16[32,208,256]{2,1,0:T(8,128)(2,1)} %bitcast.47), slice={[0:32], [0:192], [0:256]} | slice | bytes 6291456 | tf_op jit(solution)/shard_map/slice | solution.py:241
  142.4 3.7 %convert_bitcast_fusion = bf16[32,4,48,512]{3,2,0,1:T(8,128)(2,1)S(1)} fusion(bf16[32,4,48,256]{3,2,1,0:T(8,128)(2,1)} %bitcast.51, bf16[4,256,512]{2,1,0:T(8,128)(2,1)S(1)} %copy-done.6), kind=kOutput, calls=%fused_computation.5 | convolution fusion | flops 1613758464 | bytes 10485760 | tf_op jit(solution)/shard_map/dlcr,lrw->dlcw/dot_general | solution.py:247
  146.0 0.6 copy.68
  146.7 3.9 %fusion.10 = bf16[32,128,512]{2,1,0:T(8,128)(2,1)} fusion(bf16[32,192,512]{2,1,0:T(8,128)(2,1)S(1)} %bitcast.43, bf16[128]{0:T(256)(128)(2,1)S(1)} %iota_convert_fusion, bf16[32,192]{1,0:T(8,128)(2,1)S(1)} %eq.83), kind=kOutput, calls=%fused_computation.12 | convolution fusion | flops 808189952 | bytes 10498304 | tf_op jit(solution)/shard_map/dts,dsw->dtw/dot_general | solution.py:249
  150.7 4.5 %fusion.6 = bf16[32,192,512]{2,1,0:T(8,128)(2,1)S(1)} fusion(bf16[32,128,512]{2,1,0:T(8,128)(2,1)} %all-gather.3.cloned.1.call-done, bf16[128]{0:T(256)(128)(2,1)S(1)} %iota_convert_fusion, bf16[32,192]{1,0:T(8,128)(2,1)S(1)} %eq.83), kind=kOutput, calls=%fused_computation.10 | convolution fusion | flops 809238528 | bytes 10498304 | tf_op jit(solution)/shard_map/dts,dtw->dsw/dot_general | solution.py:255
  155.2 1.8 bitcast_convert_fusion
  157.0 17.0 %all_to_all.16 = bf16[8,128,512]{2,1,0:T(8,128)(2,1)S(1)} all-to-all(bf16[8,128,512]{2,1,0:T(8,128)(2,1)S(1)} %bitcast.56), channel_id=1, replica_groups=mesh['far'=4,'near'=4,'dp'=2] {'near','dp'}, dimensions={0} | all-to-all | bytes 2097152 | tf_op jit(solution)/shard_map/all_to_all | solution.py:259
  174.0 55.1 %reduce-scatter.2.cloned.1.call-done = bf16[1,8,128,512]{3,2,1,0:T(8,128)(2,1)} async-done(((bf16[4,8,128,512]{3,2,1,0:T(8,128)(2,1)}), bf16[1,8,128,512]{3,2,1,0:T(8,128)(2,1)}) %reduce-scatter.2.cloned.1.call-update) | async-done | bytes 1048592 | tf_op jit(solution)/shard_map/reduce_scatter | solution.py:251
  229.1 3.6 %all-to-all-start = ((bf16[8,128,512]{2,1,0:T(8,128)(2,1)}), bf16[8,128,512]{2,1,0:T(8,128)(2,1)S(1)}, u32[]{:S(2)}, u32[]{:S(2)}) async-start(bf16[8,128,512]{2,1,0:T(8,128)(2,1)} %bitcast.53), calls=%async_computation.1 | async-start | bytes 2097152 | tf_op jit(solution)/shard_map/all_to_all | solution.py:252
  232.7 1.1 copy.76
  233.8 13.4 %all-to-all-done = bf16[8,128,512]{2,1,0:T(8,128)(2,1)S(1)} async-done(((bf16[8,128,512]{2,1,0:T(8,128)(2,1)}), bf16[8,128,512]{2,1,0:T(8,128)(2,1)S(1)}, u32[]{:S(2)}, u32[]{:S(2)}) %all-to-all-start) | async-done | bytes 1048608 | tf_op jit(solution)/shard_map/all_to_all | solution.py:252
  247.3 1.1 copy.75
  (38 shorter events, 2.1 us)
Async XLA Ops:
  7.2 75.4 %copy-start = (bf16[128,4096]{1,0:T(8,128)(2,1)S(1)}, bf16[128,4096]{1,0:T(8,128)(2,1)}, u32[]{:S(2)}) copy-start(bf16[128,4096]{1,0:T(8,128)(2,1)} %param.7) | copy-start | bytes 3145732
  7.2 22.6 %copy-start.5 = (s32[128,4]{0,1:T(4,128)S(1)}, s32[128,4]{0,1:T(4,128)}, u32[]{:S(2)}) copy-start(s32[128,4]{0,1:T(4,128)} %param.8) | copy-start | bytes 6148
  7.2 23.1 %copy-start.3 = (s32[128,4,32]{0,2,1:T(8,128)S(1)}, s32[128,4,32]{0,2,1:T(8,128)}, u32[]{:S(2)}) copy-start(s32[128,4,32]{0,2,1:T(8,128)} %param.9) | copy-start | bytes 196612
  7.2 23.2 %copy-start.4 = (bf16[256,512]{1,0:T(8,128)(2,1)S(1)}, bf16[256,512]{1,0:T(8,128)(2,1)}, u32[]{:S(2)}) copy-start(bf16[256,512]{1,0:T(8,128)(2,1)} %param.10) | copy-start | bytes 786436
  7.2 143.5 %all-gather.3.cloned.1.call-start = ((), (), s32[]{:S(2)}) async-start(), calls=%async_computation.5 | async-start | bytes 5242880 | tf_op jit(solution)/shard_map/all_gather | solution.py:201
  29.7 199.4 %reduce-scatter.2.cloned.1.call-start = ((), (), s32[]{:S(2)}) async-start(), calls=%async_computation.4 | async-start | bytes 5242880 | tf_op jit(solution)/shard_map/reduce_scatter | solution.py:251
  30.0 56.1 %copy-start.2 = (bf16[4,256,128]{2,1,0:T(8,128)(2,1)S(1)}, bf16[4,256,128]{2,1,0:T(8,128)(2,1)}, u32[]{:S(2)}) copy-start(bf16[4,256,128]{2,1,0:T(8,128)(2,1)} %param.11) | copy-start | bytes 786436
  100.8 41.6 %copy-start.6 = (bf16[4,256,512]{2,1,0:T(8,128)(2,1)S(1)}, bf16[4,256,512]{2,1,0:T(8,128)(2,1)}, u32[]{:S(2)}) copy-start(bf16[4,256,512]{2,1,0:T(8,128)(2,1)} %get-tuple-element.5) | copy-start | bytes 3145732
  150.7 4.5 %copy-start.1 = (bf16[32,192,256]{2,1,0:T(8,128)(2,1)S(1)}, bf16[32,192,256]{2,1,0:T(8,128)(2,1)}, u32[]{:S(2)}) copy-start(bf16[32,192,256]{2,1,0:T(8,128)(2,1)} %slice.9) | copy-start | bytes 9437188
  229.1 18.2 %all-to-all-start = ((bf16[8,128,512]{2,1,0:T(8,128)(2,1)}), bf16[8,128,512]{2,1,0:T(8,128)(2,1)S(1)}, u32[]{:S(2)}, u32[]{:S(2)}) async-start(bf16[8,128,512]{2,1,0:T(8,128)(2,1)} %bitcast.53), calls=%async_computation.1 | async-start | bytes 2097152 | tf_op jit(solution)/shard_map/all_to_all | solution.py:252
Sparse Core Ops, SparseCore 0:
  29.8 96.3 all-gather.2
  150.8 78.2 reduce-scatter.1

commit v3 on v2

--- a/solution.py
+++ b/solution.py
@@ -53,10 +53,13 @@
     return found
 
 
-def spread(me, sizes, plans, own, slot, started, send_sem, recv_sem):
+def spread(me, sizes, plans, own, slot, started, send_sem, recv_sem, events=()):
     pending = {}
     longest = max(len(nodes) for nodes in plans)
     for number in range(longest):
+        for when, event in events:
+            if when == number:
+                event()
         for item, nodes in enumerate(plans):
             if number >= len(nodes):
                 continue
@@ -80,12 +83,37 @@
                 started.append(copy)
 
 
-def gather_kernel(sizes, qw_ref, val_ref, out_ref, vals_ref, send_sem, recv_sem, vsend, vrecv):
+def rank_in_layer(spot, sizes):
+    return (spot[1] * 2 + spot[2]) * sizes[3] + spot[3]
+
+
+def layer_peers(me, sizes):
+    layer = sizes[1] * sizes[2] * sizes[3]
+    mine = rank_in_layer(me, sizes)
+    for r in range(1, layer):
+        j = lax.rem(mine + r, layer)
+        near = j // sizes[3]
+        yield r - 1, j, (me[0], near // 2, near % 2, lax.rem(j, sizes[3]))
+
+
+def columns(j, part):
+    return pl.ds(pl.multiple_of(j * part, part), part)
+
+
+def gather_kernel(
+    sizes, qw_ref, val_ref, cot_ref, out_ref, vals_ref, hop_ref,
+    send_sem, recv_sem, vsend, vrecv, csend, crecv, hsend, hrecv, local,
+):
     me = place()
+    far = sizes[0]
+    z = me[0]
+    mine = rank_in_layer(me, sizes)
+    width = hop_ref.shape[3]
     half = qw_ref.shape[0] // 2
     part = vals_ref.shape[2]
     corner = (0, 1, 1, 0)
-    greet([moved(me, sizes, s) for s in steps(sizes) + [corner]])
+    beside = [moved(me, sizes, s) for s in steps((far, 1, 1, 1))]
+    greet(beside + [spot for _, _, spot in layer_peers(me, sizes)])
     for item in range(2):
         out_ref[me[0], me[1], me[2], me[3], item] = qw_ref[pl.ds(item * half, half), :]
     started = []
@@ -96,8 +124,47 @@
     def slot(item, spot):
         return out_ref.at[spot[0], spot[1], spot[2], spot[3], item]
 
+    cuts = []
+
+    def hop(side):
+        return pltpu.make_async_remote_copy(
+            src_ref=hop_ref.at[0],
+            dst_ref=hop_ref.at[1 + side],
+            send_sem=hsend.at[side],
+            recv_sem=hrecv.at[side],
+            device_id=device((z + 1 - 2 * side,) + me[1:]),
+            device_id_type=MESH,
+        )
+
+    def cut():
+        for number, j, spot in layer_peers(me, sizes):
+            copy = pltpu.make_async_remote_copy(
+                src_ref=cot_ref.at[:, columns(j, width)],
+                dst_ref=hop_ref.at[0, mine],
+                send_sem=csend.at[number],
+                recv_sem=crecv.at[number],
+                device_id=device(spot),
+                device_id_type=MESH,
+            )
+            copy.start()
+            cuts.append(copy)
+        keep = pltpu.make_async_copy(
+            cot_ref.at[:, columns(mine, width)], hop_ref.at[0, mine], local
+        )
+        keep.start()
+        cuts.append(keep)
+
+    def forward():
+        for copy in cuts[:-1]:
+            copy.wait_recv()
+        cuts[-1].wait()
+        pl.when(z < far - 1)(lambda: hop(0).start())
+        pl.when(z > 0)(lambda: hop(1).start())
+
     plans = [tree(order, sizes) for order in ORDERS]
-    spread(me, sizes, plans, own, slot, started, send_sem, recv_sem)
+    events = ((1, cut), (12, forward))
+    spread(me, sizes, plans, own, slot, started, send_sem, recv_sem, events)
+    started.extend(cuts[:-1])
     pushes = []
     for number, step in enumerate(((0, 1, 0, 0), (0, 0, 1, 0), corner)):
         peer = moved(me, sizes, step)
@@ -118,6 +185,160 @@
         copy.wait_send()
     for copy in pushes:
         copy.wait()
+    pl.when(z < far - 1)(lambda: hop(0).wait_send())
+    pl.when(z > 0)(lambda: hop(0).wait_recv())
+    pl.when(z > 0)(lambda: hop(1).wait_send())
+    pl.when(z < far - 1)(lambda: hop(1).wait_recv())
+
+
+def push_layer(me, sizes, source, target, send_sem, recv_sem):
+    mine = rank_in_layer(me, sizes)
+    part = source.shape[2]
+    copies = []
+    for number, j, spot in layer_peers(me, sizes):
+        copy = pltpu.make_async_remote_copy(
+            src_ref=source.at[j],
+            dst_ref=target.at[:, columns(mine, part)],
+            send_sem=send_sem.at[number],
+            recv_sem=recv_sem.at[number],
+            device_id=device(spot),
+            device_id_type=MESH,
+        )
+        copy.start()
+        copies.append(copy)
+    target[:, columns(mine, part)] = source[mine]
+    for copy in copies:
+        copy.wait()
+
+
+def push_kernel(sizes, grad_ref, out_ref, send_sem, recv_sem):
+    me = place()
+    greet([spot for _, _, spot in layer_peers(me, sizes)])
+    push_layer(me, sizes, grad_ref, out_ref, send_sem, recv_sem)
+
+
+def line_kernel(
+    sizes, part_ref, hop_ref, out_ref, cot_ref, sums, total,
+    ssend, srecv, hsend, hrecv, csend, crecv, local,
+):
+    me = place()
+    far = sizes[0]
+    z = me[0]
+    beside = [moved(me, sizes, s) for s in steps((far, 1, 1, 1))]
+    greet(beside + [spot for _, _, spot in layer_peers(me, sizes)])
+    near = ((0, z), (1, z - 1), (2, z + 1))
+    inside = (z >= 0, z > 0, z < far - 1)
+
+    def keep(k):
+        return pltpu.make_async_copy(hop_ref.at[k], cot_ref.at[near[k][1]], local.at[k])
+
+    for k in range(3):
+        pl.when(inside[k])(lambda k=k: keep(k).start())
+
+    def where(side):
+        return z if side == 0 else far - 1 - z
+
+    def toward(side):
+        return device((z + 1 - 2 * side,) + me[1:])
+
+    def goal(side, s):
+        return far - 1 - s + z if side == 0 else s - far + 1 + z
+
+    def summed(side, s, first):
+        d = goal(side, s)
+        return pltpu.make_async_remote_copy(
+            src_ref=part_ref.at[d] if first else sums.at[side, d],
+            dst_ref=sums.at[side, d],
+            send_sem=ssend.at[side, s],
+            recv_sem=srecv.at[side, s],
+            device_id=toward(side),
+            device_id_type=MESH,
+        )
+
+    def arrived(side, s):
+        d = goal(side, s + 1)
+        return pltpu.make_async_remote_copy(
+            src_ref=sums.at[side, d],
+            dst_ref=sums.at[side, d],
+            send_sem=ssend.at[side, s],
+            recv_sem=srecv.at[side, s],
+            device_id=toward(side),
+            device_id_type=MESH,
+        )
+
+    def passed(side, h):
+        c = z - (h - 1) if side == 0 else z + (h - 1)
+        return pltpu.make_async_remote_copy(
+            src_ref=hop_ref.at[1 + side] if h == 2 else cot_ref.at[c],
+            dst_ref=cot_ref.at[c],
+            send_sem=hsend.at[side, h],
+            recv_sem=hrecv.at[side, h],
+            device_id=toward(side),
+            device_id_type=MESH,
+        )
+
+    def came(side, h):
+        c = z - h if side == 0 else z + h
+        return pltpu.make_async_remote_copy(
+            src_ref=cot_ref.at[c],
+            dst_ref=cot_ref.at[c],
+            send_sem=hsend.at[side, h],
+            recv_sem=hrecv.at[side, h],
+            device_id=toward(side),
+            device_id_type=MESH,
+        )
+
+    def add(side, s):
+        d = goal(side, s)
+
+        @pl.loop(0, sums.shape[2])
+        def _(j):
+            here = sums[side, d, j].astype(jnp.float32) + part_ref[d, j].astype(jnp.float32)
+            sums[side, d, j] = here.astype(sums.dtype)
+
+    for s in range(far - 1):
+        for side in range(2):
+            pl.when(where(side) == 0)(lambda: summed(side, s, True).start())
+            if s:
+
+                @pl.when((where(side) > 0) & (where(side) <= s))
+                def _():
+                    arrived(side, s - 1).wait_recv()
+                    add(side, s)
+                    summed(side, s, False).start()
+
+        h = s + 2
+        if h < far:
+            for side in range(2):
+                if h > 2:
+                    pl.when(where(side) >= h - 1)(lambda: came(side, h - 1).wait_recv())
+                active = (where(side) >= h - 1) & (where(side) < far - 1)
+                pl.when(active)(lambda: passed(side, h).start())
+
+    for side in range(2):
+        pl.when(where(side) > 0)(lambda: arrived(side, far - 2).wait_recv())
+
+    @pl.loop(0, total.shape[0])
+    def _(j):
+        here = part_ref[z, j].astype(jnp.float32)
+        up = jnp.where(z > 0, sums[0, z, j].astype(jnp.float32), 0.0)
+        down = jnp.where(z < far - 1, sums[1, z, j].astype(jnp.float32), 0.0)
+        total[j] = (here + up + down).astype(total.dtype)
+
+    push_layer(me, sizes, total, out_ref, csend, crecv)
+    for side in range(2):
+        for s in range(far - 1):
+            pl.when(where(side) == 0)(lambda: summed(side, s, True).wait_send())
+            if s:
+                busy = (where(side) > 0) & (where(side) <= s)
+                pl.when(busy)(lambda: summed(side, s, False).wait_send())
+        for h in range(2, far):
+            active = (where(side) >= h - 1) & (where(side) < far - 1)
+            pl.when(active)(lambda: passed(side, h).wait_send())
+        if far > 2:
+            pl.when(where(side) >= far - 1)(lambda: came(side, far - 1).wait_recv())
+    for k in range(3):
+        pl.when(inside[k])(lambda k=k: keep(k).wait())
 
 
 def table_kernel(sizes, send_ref, out_ref, send_sem, recv_sem):
@@ -142,25 +363,71 @@
 VMEM = pl.BlockSpec(memory_space=pltpu.VMEM)
 
 
-def gather(sizes, mine, values, near, part):
+def gather(sizes, mine, values, cotangent, near, part):
+    layer = near * sizes[3]
     count = sizes[0] * sizes[1] * sizes[2] * sizes[3]
     return pl.pallas_call(
         functools.partial(gather_kernel, sizes),
         out_shape=(
             jax.ShapeDtypeStruct(sizes + (2, mine.shape[0] // 2, mine.shape[1]), mine.dtype),
             jax.ShapeDtypeStruct((near, values.shape[0], part), values.dtype),
+            jax.ShapeDtypeStruct((3, layer, cotangent.shape[0], part), cotangent.dtype),
         ),
-        in_specs=[VMEM] * 2,
-        out_specs=(VMEM, VMEM),
+        in_specs=[VMEM] * 3,
+        out_specs=(VMEM, VMEM, VMEM),
         scratch_shapes=[
             pltpu.SemaphoreType.DMA((2, count)),
             pltpu.SemaphoreType.DMA((2, count)),
             pltpu.SemaphoreType.DMA((3,)),
             pltpu.SemaphoreType.DMA((3,)),
+            pltpu.SemaphoreType.DMA((layer,)),
+            pltpu.SemaphoreType.DMA((layer,)),
+            pltpu.SemaphoreType.DMA((2,)),
+            pltpu.SemaphoreType.DMA((2,)),
+            pltpu.SemaphoreType.DMA,
         ],
         compiler_params=pltpu.CompilerParams(collective_id=0, has_side_effects=True),
         name="gather_rows",
-    )(mine, values)
+    )(mine, values, cotangent)
+
+
+def push(sizes, grad):
+    layer, rows, part = grad.shape
+    return pl.pallas_call(
+        functools.partial(push_kernel, sizes),
+        out_shape=jax.ShapeDtypeStruct((rows, layer * part), grad.dtype),
+        in_specs=[VMEM],
+        out_specs=VMEM,
+        scratch_shapes=[pltpu.SemaphoreType.DMA((layer,)), pltpu.SemaphoreType.DMA((layer,))],
+        compiler_params=pltpu.CompilerParams(collective_id=2, has_side_effects=True),
+        name="push_gradient",
+    )(grad)
+
+
+def line(sizes, partial, hops):
+    far, layer, rows, part = partial.shape
+    return pl.pallas_call(
+        functools.partial(line_kernel, sizes),
+        out_shape=(
+            jax.ShapeDtypeStruct((rows, layer * part), partial.dtype),
+            jax.ShapeDtypeStruct((far,) + hops.shape[1:], hops.dtype),
+        ),
+        in_specs=[VMEM] * 2,
+        out_specs=(VMEM, VMEM),
+        scratch_shapes=[
+            pltpu.VMEM((2,) + partial.shape, partial.dtype),
+            pltpu.VMEM(partial.shape[1:], partial.dtype),
+            pltpu.SemaphoreType.DMA((2, far)),
+            pltpu.SemaphoreType.DMA((2, far)),
+            pltpu.SemaphoreType.DMA((2, far)),
+            pltpu.SemaphoreType.DMA((2, far)),
+            pltpu.SemaphoreType.DMA((layer,)),
+            pltpu.SemaphoreType.DMA((layer,)),
+            pltpu.SemaphoreType.DMA((3,)),
+        ],
+        compiler_params=pltpu.CompilerParams(collective_id=3, has_side_effects=True),
+        name="sum_line",
+    )(partial, hops)
 
 
 def exchange(sizes, send):
@@ -196,14 +463,10 @@
     f32, bf16 = jnp.float32, jnp.bfloat16
     y = lax.axis_index("dp")
 
-    cot = cotangent.reshape(tok_rows, layer, part).transpose(1, 0, 2)
-    cot = lax.all_to_all(cot, ("near", "dp"), split_axis=0, concat_axis=0, tiled=True)
-    cot = lax.all_gather(cot, "far", axis=0, tiled=False)
-
     own = query_weight.shape[0] // copies
     mine = lax.dynamic_slice_in_dim(query_weight, y * own, own, axis=0)
     sizes = (far, 2, near // 2, copies)
-    qw, vals = gather(sizes, mine, values, near, part)
+    qw, vals, hops = gather(sizes, mine, values, cotangent, near, part)
     qw = qw.reshape(width, -1)
     query = jnp.dot(tokens, qw, preferred_element_type=f32).astype(bf16)
     query = query.reshape(tok_rows, heads, key_width)
@@ -242,22 +505,19 @@
     who = got[:, near * capacity : near * capacity + near, :capacity]
     pick = (who[:, None, :, :] == row.astype(bf16)[None, :, None, None]).astype(bf16)
     pick = pick.reshape(far * layer, tok_rows, near * capacity)
-    cot = cot.reshape(far * layer, tok_rows, part)
 
     reads = jnp.einsum("dlcr,lrw->dlcw", slots, vals, preferred_element_type=f32).astype(bf16)
     reads = reads.reshape(far * layer, near * capacity, part)
     partial = jnp.einsum("dts,dsw->dtw", pick, reads, preferred_element_type=f32).astype(bf16)
     partial = partial.reshape(far, layer, tok_rows, part)
-    total = lax.psum_scatter(partial, "far", scatter_dimension=0, tiled=False)
-    total = lax.all_to_all(total, ("near", "dp"), split_axis=0, concat_axis=0, tiled=True)
-    memory_out = total.transpose(1, 0, 2).reshape(tok_rows, width)
+    memory_out, cot = line(sizes, partial, hops)
+    cot = cot.reshape(far * layer, tok_rows, part)
 
     terms = jnp.einsum("dts,dtw->dsw", pick, cot, preferred_element_type=f32).astype(bf16)
     terms = terms.reshape(far * layer, near, capacity, part)
     grad = jnp.einsum("dlcr,dlcw->lrw", slots, terms, preferred_element_type=f32).astype(bf16)
     grad = grad.reshape(layer, block_rows // copies, part)
-    grad = lax.all_to_all(grad, ("near", "dp"), split_axis=0, concat_axis=0, tiled=True)
-    grad_values = grad.transpose(1, 0, 2).reshape(block_rows // copies, width)
+    grad_values = push(sizes, grad)
     return memory_out, grad_values
 
 

time: 256 us -> 239 us (0.934)
  Pallas kernels: 88.1 us -> 192 us
  waiting for transfers between devices: 68.6 us -> 0 us
  blocking collectives: 36.4 us -> 0 us
  between operations: 14.4 us -> 0.9 us
  starting transfers between devices: 3.71 us -> 0 us
    pallas_call x0 -> x2, Pallas kernels: none -> 108 us  [the longest x1 91.5 us: line(): pl.pallas_call(functools.partial(line_kernel, sizes), out_shape=(jax.Shap...]
    reduce_scatter x1 -> x0, waiting for transfers between devices: 55.1 us -> none  [body(): total = lax.psum_scatter(partial, 'far', scatter_dimension=0, tiled=False)]
    all_to_all x2 -> x0, blocking collectives: 36.4 us -> none  [the longest x1 19.4 us: body(): lax.all_to_all(cot, ('near', 'dp'), split_axis=0, concat_axis=0, tiled=True)]
    all_to_all x1 -> x0, waiting for transfers between devices: 13.4 us -> none  [body(): lax.all_to_all(total, ('near', 'dp'), split_axis=0, concat_axis=0, tiled=...]
    pallas_call x1, Pallas kernels: 36.6 us -> 27.2 us  [exchange(): pl.pallas_call(functools.partial(table_kernel, sizes), out_shape=jax.Shap...]
    pallas_call x1, Pallas kernels: 51.5 us -> 56.3 us  [gather(): pl.pallas_call(functools.partial(gather_kernel, sizes), out_shape=(jax.Sh...]
    all_to_all x1 -> x0, starting transfers between devices: 3.63 us -> none  [body(): lax.all_to_all(total, ('near', 'dp'), split_axis=0, concat_axis=0, tiled=...]
  transfers between devices with their start and end apart: 3 -> 0, of which waited for: 2 -> 0; matrix products, arithmetic and copies ran while one was open for 16% -> 0% of each run, Pallas kernels for 35% -> 0%
where the time goes in v3:
time: 239 us
  Pallas kernels  192 us (80%)
  matrix products  19.1 us (8%)
  other arithmetic  14.6 us (6%)
  local copies, waits for them, and re-layouts  12.3 us (5%)
    pallas_call x1, Pallas kernels, line(): pl.pallas_call(functools.partial(line_kernel, sizes), out_shape=(jax.Shap...  91.5 us
    pallas_call x1, Pallas kernels, gather(): pl.pallas_call(functools.partial(gather_kernel, sizes), out_shape=(jax.Sh...  56.3 us
    pallas_call x1, Pallas kernels, exchange(): pl.pallas_call(functools.partial(table_kernel, sizes), out_shape=jax.Shap...  27.2 us
    pallas_call x1, Pallas kernels, push(): pl.pallas_call(functools.partial(push_kernel, sizes), out_shape=jax.Shape...  16.8 us
    reduce_sum x1, other arithmetic, body(): jnp.sum(jnp.where(match, weight.astype(f32)[:, :, :, None], 0.0), axis=2)  6.6 us
    reduce_sum x1, other arithmetic, body(): picked = jnp.sum(jnp.where(match, full[:, :, None, :], 0.0), axis=3)  5.32 us

profile of v3, /device:TPU:0, one launch (start us, length us, event | category | flops | bytes accessed | tf_op | source)
XLA Modules:
  0.0 238.8 jit_solution(15765725285534652019)
XLA Ops:
  0.7 0.8 fusion.32
  1.6 0.7 select_reduce_fusion.3
  2.3 0.3 select_reduce_fusion.2
  2.9 1.6 constant_dynamic-slice_fusion.qw_ref
  4.5 1.0 copy.39
  5.5 56.3 %gather_rows.1 = (bf16[4,2,2,2,2,64,512]{6,5,4,3,2,1,0:T(8,128)(2,1)}, bf16[4,256,512]{2,1,0:T(8,128)(2,1)}, bf16[3,8,128,512]{3,2,1,0:T(8,128)(2,1)}) custom-call(bf16[128,512]{1,0:T(8,128)(2,1)} %constant_dynamic-slice_fusion.qw_ref, bf16[256,4096]{1,0:T(8,128)(2,1)} %val_ref.1, bf16[128,4096]{1,0:T(8,128)(2,1)} %cot_ref.1), custom_call_target="tpu_custom_call" | custom-call | tf_op jit(solution)/shard_map/gather_rows/pallas_call | solution.py:369
  61.8 3.5 %convolution_convert_fusion = bf16[512,128]{1,0:T(8,128)(2,1)S(1)} fusion(bf16[4096,512]{1,0:T(8,128)(2,1)} %bitcast.46, bf16[128,4096]{1,0:T(8,128)(2,1)S(1)} %copy-done), kind=kOutput, calls=%fused_computation.18 | convolution fusion | flops 536936448 | bytes 5373952 | tf_op jit(solution)/shard_map/dot_general | solution.py:471
  65.6 0.3 copy.41
  65.9 5.3 %select_reduce_fusion.1 = f32[128,4,32]{2,1,0:T(4,128)S(1)} fusion(f32[128,4,256]{2,1,0:T(4,128)S(1)} %copy.41, s32[128,4,32]{2,1,0:T(4,128)S(1)} %copy.39), kind=kLoop, calls=%fused_computation.3 | loop fusion | flops 12566528 | bytes 655360 | tf_op jit(solution)/shard_map/reduce_sum | solution.py:475
  71.6 6.6 %select_reduce_fusion = bf16[128,4,256]{2,1,0:T(4,128)(2,1)S(1)} fusion(f32[128,4,32]{2,1,0:T(4,128)S(1)} %copy.43, s32[128,4,32]{2,1,0:T(4,128)S(1)} %copy.39), kind=kLoop, calls=%fused_computation.2 | loop fusion | flops 12451840 | bytes 393216 | tf_op jit(solution)/shard_map/reduce_sum | solution.py:480
  78.3 0.4 fusion.14
  78.7 0.8 fusion.27.send_ref
  79.5 27.2 %exchange_tables.1 = bf16[4,2,2,2,208,256]{5,4,3,2,1,0:T(8,128)(2,1)} custom-call(bf16[4,208,256]{2,1,0:T(8,128)(2,1)} %fusion.27.send_ref), custom_call_target="tpu_custom_call" | custom-call | tf_op jit(solution)/shard_map/exchange_tables/pallas_call | solution.py:435
  106.7 0.9 slice.8
  107.5 4.0 %slice.9 = bf16[32,192,256]{2,1,0:T(8,128)(2,1)} slice(bf16[32,208,256]{2,1,0:T(8,128)(2,1)} %bitcast.39), slice={[0:32], [0:192], [0:256]} | slice | bytes 6291456 | tf_op jit(solution)/shard_map/slice | solution.py:504
  111.6 3.7 %convert_bitcast_fusion = bf16[32,4,48,512]{3,2,0,1:T(8,128)(2,1)S(1)} fusion(bf16[32,4,48,256]{3,2,1,0:T(8,128)(2,1)} %bitcast.40, bf16[4,256,512]{2,1,0:T(8,128)(2,1)S(1)} %copy-done.4), kind=kOutput, calls=%fused_computation.5 | convolution fusion | flops 1613758464 | bytes 10485760 | tf_op jit(solution)/shard_map/dlcr,lrw->dlcw/dot_general | solution.py:509
  115.3 0.6 copy.45
  116.0 3.9 %fusion.10 = bf16[32,128,512]{2,1,0:T(8,128)(2,1)} fusion(bf16[32,192,512]{2,1,0:T(8,128)(2,1)S(1)} %bitcast.34, bf16[128]{0:T(256)(128)(2,1)S(1)} %iota_convert_fusion, bf16[32,192]{1,0:T(8,128)(2,1)S(1)} %eq.83), kind=kOutput, calls=%fused_computation.12 | convolution fusion | flops 808189952 | bytes 10498304 | tf_op jit(solution)/shard_map/dts,dsw->dtw/dot_general | solution.py:511
  119.9 91.5 %sum_line.1 = (bf16[128,4096]{1,0:T(8,128)(2,1)}, bf16[4,8,128,512]{3,2,1,0:T(8,128)(2,1)}) custom-call(bf16[4,8,128,512]{3,2,1,0:T(8,128)(2,1)} %bitcast.36, bf16[3,8,128,512]{3,2,1,0:T(8,128)(2,1)} %get-tuple-element.9.hop_ref), custom_call_target="tpu_custom_call" | custom-call | tf_op jit(solution)/shard_map/sum_line/pallas_call | solution.py:409
  211.4 4.5 %fusion.6 = bf16[32,192,512]{2,1,0:T(8,128)(2,1)S(1)} fusion(bf16[32,128,512]{2,1,0:T(8,128)(2,1)} %bitcast.37, bf16[128]{0:T(256)(128)(2,1)S(1)} %iota_convert_fusion, bf16[32,192]{1,0:T(8,128)(2,1)S(1)} %eq.83), kind=kOutput, calls=%fused_computation.10 | convolution fusion | flops 809238528 | bytes 10498304 | tf_op jit(solution)/shard_map/dts,dtw->dsw/dot_general | solution.py:516
  215.9 2.8 %bitcast_convert_fusion = bf16[4,256,512]{2,1,0:T(8,128)(2,1)} fusion(bf16[32,4,48,256]{3,2,1,0:T(8,128)(2,1)S(1)} %bitcast.41, bf16[32,4,48,512]{3,2,1,0:T(8,128)(2,1)S(1)} %bitcast.35), kind=kOutput, calls=%fused_computation.13 | convolution fusion | flops 1611137024 | bytes 10485760 | tf_op jit(solution)/shard_map/dlcr,dlcw->lrw/dot_general | solution.py:518
  218.7 16.8 %push_gradient.1 = bf16[128,4096]{1,0:T(8,128)(2,1)} custom-call(bf16[8,128,512]{2,1,0:T(8,128)(2,1)} %bitcast.42), custom_call_target="tpu_custom_call" | custom-call | tf_op jit(solution)/shard_map/push_gradient/pallas_call | solution.py:396
  235.5 1.0 copy.52
  236.5 2.3 copy.53
  (24 shorter events, 1.1 us)
Async XLA Ops:
  0.6 61.2 %copy-start = (bf16[128,4096]{1,0:T(8,128)(2,1)S(1)}, bf16[128,4096]{1,0:T(8,128)(2,1)}, u32[]{:S(2)}) copy-start(bf16[128,4096]{1,0:T(8,128)(2,1)} %param.7) | copy-start | bytes 3145732
  5.5 59.8 %copy-start.3 = (bf16[4,256,128]{2,1,0:T(8,128)(2,1)S(1)}, bf16[4,256,128]{2,1,0:T(8,128)(2,1)}, u32[]{:S(2)}) copy-start(bf16[4,256,128]{2,1,0:T(8,128)(2,1)} %param.11) | copy-start | bytes 786436
  79.5 32.1 %copy-start.4 = (bf16[4,256,512]{2,1,0:T(8,128)(2,1)S(1)}, bf16[4,256,512]{2,1,0:T(8,128)(2,1)}, u32[]{:S(2)}) copy-start(bf16[4,256,512]{2,1,0:T(8,128)(2,1)} %get-tuple-element.8) | copy-start | bytes 3145732
  211.4 4.5 %copy-start.1 = (bf16[32,192,256]{2,1,0:T(8,128)(2,1)S(1)}, bf16[32,192,256]{2,1,0:T(8,128)(2,1)}, u32[]{:S(2)}) copy-start(bf16[32,192,256]{2,1,0:T(8,128)(2,1)} %slice.9) | copy-start | bytes 9437188
  215.9 19.7 %copy-start.2 = (bf16[128,4096]{1,0:T(8,128)(2,1)S(1)}, bf16[128,4096]{1,0:T(8,128)(2,1)}, u32[]{:S(2)}) copy-start(bf16[128,4096]{1,0:T(8,128)(2,1)} %get-tuple-element.16) | copy-start | bytes 3145732

commit v4 on v3

--- a/solution.py
+++ b/solution.py
@@ -7,6 +7,7 @@
 from jax.sharding import Mesh, PartitionSpec as P
 
 INNER = 4
+CHUNKS = 4
 MESH = pl.DeviceIdType.MESH
 AXES = ("far", "high", "low", "dp")
 ORDERS = (("far", "dp", "high", "low"), ("far", "high", "dp", "low"))
@@ -235,6 +236,35 @@
     for k in range(3):
         pl.when(inside[k])(lambda k=k: keep(k).start())
 
+    chunks = ssend.shape[2]
+    size = total.shape[0] // chunks
+    mine = rank_in_layer(me, sizes)
+    part = total.shape[2]
+
+    def chunk(q):
+        return pl.ds(q * size, size)
+
+    def give(j):
+        near, y = j // sizes[3], j % sizes[3]
+        return pltpu.make_async_remote_copy(
+            src_ref=total.at[j],
+            dst_ref=out_ref.at[:, columns(mine, part)],
+            send_sem=csend.at[j],
+            recv_sem=crecv.at[mine],
+            device_id=device((z, near // 2, near % 2, y)),
+            device_id_type=MESH,
+        )
+
+    def given(j):
+        return pltpu.make_async_remote_copy(
+            src_ref=total.at[j],
+            dst_ref=out_ref.at[:, columns(j, part)],
+            send_sem=csend.at[j],
+            recv_sem=crecv.at[j],
+            device_id=device((z, (j // sizes[3]) // 2, (j // sizes[3]) % 2, j % sizes[3])),
+            device_id_type=MESH,
+        )
+
     def where(side):
         return z if side == 0 else far - 1 - z
 
@@ -244,24 +274,24 @@
     def goal(side, s):
         return far - 1 - s + z if side == 0 else s - far + 1 + z
 
-    def summed(side, s, first):
+    def summed(side, s, first, q):
         d = goal(side, s)
         return pltpu.make_async_remote_copy(
-            src_ref=part_ref.at[d] if first else sums.at[side, d],
-            dst_ref=sums.at[side, d],
-            send_sem=ssend.at[side, s],
-            recv_sem=srecv.at[side, s],
+            src_ref=part_ref.at[d, chunk(q)] if first else sums.at[side, d, chunk(q)],
+            dst_ref=sums.at[side, d, chunk(q)],
+            send_sem=ssend.at[side, s, q],
+            recv_sem=srecv.at[side, s, q],
             device_id=toward(side),
             device_id_type=MESH,
         )
 
-    def arrived(side, s):
+    def arrived(side, s, q):
         d = goal(side, s + 1)
         return pltpu.make_async_remote_copy(
-            src_ref=sums.at[side, d],
-            dst_ref=sums.at[side, d],
-            send_sem=ssend.at[side, s],
-            recv_sem=srecv.at[side, s],
+            src_ref=sums.at[side, d, chunk(q)],
+            dst_ref=sums.at[side, d, chunk(q)],
+            send_sem=ssend.at[side, s, q],
+            recv_sem=srecv.at[side, s, q],
             device_id=toward(side),
             device_id_type=MESH,
         )
@@ -288,24 +318,25 @@
             device_id_type=MESH,
         )
 
-    def add(side, s):
+    def add(side, s, q):
         d = goal(side, s)
 
-        @pl.loop(0, sums.shape[2])
+        @pl.loop(q * size, (q + 1) * size)
         def _(j):
             here = sums[side, d, j].astype(jnp.float32) + part_ref[d, j].astype(jnp.float32)
             sums[side, d, j] = here.astype(sums.dtype)
 
     for s in range(far - 1):
-        for side in range(2):
-            pl.when(where(side) == 0)(lambda: summed(side, s, True).start())
-            if s:
-
-                @pl.when((where(side) > 0) & (where(side) <= s))
-                def _():
-                    arrived(side, s - 1).wait_recv()
-                    add(side, s)
-                    summed(side, s, False).start()
+        for q in range(chunks):
+            for side in range(2):
+                pl.when(where(side) == 0)(lambda: summed(side, s, True, q).start())
+                if s:
+
+                    @pl.when((where(side) > 0) & (where(side) <= s))
+                    def _():
+                        arrived(side, s - 1, q).wait_recv()
+                        add(side, s, q)
+                        summed(side, s, False, q).start()
 
         h = s + 2
         if h < far:
@@ -315,23 +346,31 @@
                 active = (where(side) >= h - 1) & (where(side) < far - 1)
                 pl.when(active)(lambda: passed(side, h).start())
 
-    for side in range(2):
-        pl.when(where(side) > 0)(lambda: arrived(side, far - 2).wait_recv())
-
-    @pl.loop(0, total.shape[0])
-    def _(j):
-        here = part_ref[z, j].astype(jnp.float32)
-        up = jnp.where(z > 0, sums[0, z, j].astype(jnp.float32), 0.0)
-        down = jnp.where(z < far - 1, sums[1, z, j].astype(jnp.float32), 0.0)
-        total[j] = (here + up + down).astype(total.dtype)
-
-    push_layer(me, sizes, total, out_ref, csend, crecv)
+    for q in range(chunks):
+        for side in range(2):
+            pl.when(where(side) > 0)(lambda: arrived(side, far - 2, q).wait_recv())
+
+        @pl.loop(q * size, (q + 1) * size)
+        def _(j):
+            here = part_ref[z, j].astype(jnp.float32)
+            up = jnp.where(z > 0, sums[0, z, j].astype(jnp.float32), 0.0)
+            down = jnp.where(z < far - 1, sums[1, z, j].astype(jnp.float32), 0.0)
+            total[j] = (here + up + down).astype(total.dtype)
+
+        for j in range(q * size, (q + 1) * size):
+            pl.when(mine != j)(lambda: give(j).start())
+
+    out_ref[:, columns(mine, part)] = total[mine]
+    for j in range(total.shape[0]):
+        pl.when(mine != j)(lambda: give(j).wait_send())
+        pl.when(mine != j)(lambda: given(j).wait_recv())
     for side in range(2):
         for s in range(far - 1):
-            pl.when(where(side) == 0)(lambda: summed(side, s, True).wait_send())
-            if s:
-                busy = (where(side) > 0) & (where(side) <= s)
-                pl.when(busy)(lambda: summed(side, s, False).wait_send())
+            for q in range(chunks):
+                pl.when(where(side) == 0)(lambda: summed(side, s, True, q).wait_send())
+                if s:
+                    busy = (where(side) > 0) & (where(side) <= s)
+                    pl.when(busy)(lambda: summed(side, s, False, q).wait_send())
         for h in range(2, far):
             active = (where(side) >= h - 1) & (where(side) < far - 1)
             pl.when(active)(lambda: passed(side, h).wait_send())
@@ -341,20 +380,25 @@
         pl.when(inside[k])(lambda k=k: keep(k).wait())
 
 
-def table_kernel(sizes, send_ref, out_ref, send_sem, recv_sem):
+def table_kernel(sizes, send_ref, who_ref, out_ref, whose_ref, send_sem, recv_sem):
     me = place()
     half = send_ref.shape[2] // 2
     greet([moved(me, sizes, s) for s in steps(sizes)])
     out_ref[me[0], me[1], me[2], me[3]] = send_ref[me[0]]
+    whose_ref[me[0], me[1], me[2], me[3]] = who_ref[me[0]]
     started = []
 
     def own(item, axis, peer):
-        return send_ref.at[peer[0], :, pl.ds(item * half, half)]
+        if item == 0:
+            return who_ref.at[peer[0]]
+        return send_ref.at[peer[0], :, pl.ds((item - 1) * half, half)]
 
     def slot(item, spot):
-        return out_ref.at[spot[0], spot[1], spot[2], spot[3], :, pl.ds(item * half, half)]
-
-    plans = [tree(order, sizes) for order in ORDERS]
+        if item == 0:
+            return whose_ref.at[spot[0], spot[1], spot[2], spot[3]]
+        return out_ref.at[spot[0], spot[1], spot[2], spot[3], :, pl.ds((item - 1) * half, half)]
+
+    plans = [tree(order, sizes) for order in ORDERS[:1] + ORDERS]
     spread(me, sizes, plans, own, slot, started, send_sem, recv_sem)
     for copy in started:
         copy.wait_send()
@@ -417,8 +461,8 @@
         scratch_shapes=[
             pltpu.VMEM((2,) + partial.shape, partial.dtype),
             pltpu.VMEM(partial.shape[1:], partial.dtype),
-            pltpu.SemaphoreType.DMA((2, far)),
-            pltpu.SemaphoreType.DMA((2, far)),
+            pltpu.SemaphoreType.DMA((2, far, CHUNKS)),
+            pltpu.SemaphoreType.DMA((2, far, CHUNKS)),
             pltpu.SemaphoreType.DMA((2, far)),
             pltpu.SemaphoreType.DMA((2, far)),
             pltpu.SemaphoreType.DMA((layer,)),
@@ -430,20 +474,23 @@
     )(partial, hops)
 
 
-def exchange(sizes, send):
+def exchange(sizes, send, who):
     count = sizes[0] * sizes[1] * sizes[2] * sizes[3]
     return pl.pallas_call(
         functools.partial(table_kernel, sizes),
-        out_shape=jax.ShapeDtypeStruct(sizes + send.shape[1:], send.dtype),
-        in_specs=[VMEM],
-        out_specs=VMEM,
+        out_shape=(
+            jax.ShapeDtypeStruct(sizes + send.shape[1:], send.dtype),
+            jax.ShapeDtypeStruct(sizes + who.shape[1:], who.dtype),
+        ),
+        in_specs=[VMEM] * 2,
+        out_specs=(VMEM, VMEM),
         scratch_shapes=[
-            pltpu.SemaphoreType.DMA((2, count)),
-            pltpu.SemaphoreType.DMA((2, count)),
+            pltpu.SemaphoreType.DMA((3, count)),
+            pltpu.SemaphoreType.DMA((3, count)),
         ],
         compiler_params=pltpu.CompilerParams(collective_id=1, has_side_effects=True),
         name="exchange_tables",
-    )(send)
+    )(send, who)
 
 
 def body(tokens, owner, row_pick, query_weight, sub_keys, values, cotangent):
@@ -472,13 +519,11 @@
     query = query.reshape(tok_rows, heads, key_width)
     full = jnp.einsum("thk,hrk->thr", query, sub_keys, preferred_element_type=f32)
     match = row_pick[:, :, :, None] == jnp.arange(block_rows, dtype=jnp.int32)[None, None, None, :]
-    picked = jnp.sum(jnp.where(match, full[:, :, None, :], 0.0), axis=3)
-    score = picked * (1.0 / key_width**0.5)
+    score = jnp.where(jnp.any(match, axis=2), full * (1.0 / key_width**0.5), -jnp.inf)
     top = jnp.max(score, axis=2, keepdims=True)
     expo = jnp.exp(score - top)
     weight = (expo / jnp.sum(expo, axis=2, keepdims=True)).astype(bf16)
-    table = jnp.sum(jnp.where(match, weight.astype(f32)[:, :, :, None], 0.0), axis=2)
-    table = table.astype(bf16).reshape(requests, block_rows)
+    table = weight.reshape(requests, block_rows)
 
     ids = jnp.arange(groups, dtype=jnp.int32)
     hits = owner[:, :, None] == ids[None, None, :]
@@ -496,13 +541,12 @@
     send = send.reshape(groups, capacity, block_rows)
     held = named[:, :, None] & (rank[:, :, None] == places)
     who = jnp.sum(jnp.where(held, row[:, None, None] + 1, 0), axis=0) - 1
-    spare = 16 * -(-near // 16)
+    lanes = 128 * -(-capacity // 128)
     who = who.astype(bf16).reshape(far, near, capacity)
-    who = jnp.pad(who, ((0, 0), (0, spare - near), (0, block_rows - capacity)))
-    send = jnp.concatenate([send.reshape(far, near * capacity, block_rows), who], axis=1)
-    got = exchange(sizes, send).reshape(far * layer, near * capacity + spare, block_rows)
-    slots = got[:, : near * capacity].reshape(far * layer, near, capacity, block_rows)
-    who = got[:, near * capacity : near * capacity + near, :capacity]
+    who = jnp.pad(who, ((0, 0), (0, 16 * -(-near // 16) - near), (0, lanes - capacity)))
+    slots, who = exchange(sizes, send.reshape(far, near * capacity, block_rows), who)
+    slots = slots.reshape(far * layer, near, capacity, block_rows)
+    who = who.reshape((far * layer,) + who.shape[4:])[:, :near, :capacity]
     pick = (who[:, None, :, :] == row.astype(bf16)[None, :, None, None]).astype(bf16)
     pick = pick.reshape(far * layer, tok_rows, near * capacity)
 

time: 239 us -> 224 us (0.937)
  other arithmetic: 14.6 us -> 7.54 us
  Pallas kernels: 192 us -> 187 us
  local copies, waits for them, and re-layouts: 12.3 us -> 8.54 us
    reduce_sum x2 -> x0, other arithmetic: 11.9 us -> none  [the longest x1 6.6 us: body(): jnp.sum(jnp.where(match, weight.astype(f32)[:, :, :, None], 0.0), axis=2)]
    pallas_call x1, Pallas kernels: 91.5 us -> 85.3 us  [line(): pl.pallas_call(functools.partial(line_kernel, sizes), out_shape=(jax.Shap...]
    reduce_or x0 -> x1, other arithmetic: none -> 5.54 us  [body(): jnp.any(match, axis=2)]
    slice x2 -> x1, local copies, waits for them, and re-layouts: 4.83 us -> 0.85 us  [body(): who = who.reshape((far * layer,) + who.shape[4:])[:, :near, :capacity]]
where the time goes in v4:
time: 224 us
  Pallas kernels  187 us (83%)
  matrix products  20.2 us (9%)
  local copies, waits for them, and re-layouts  8.54 us (4%)
  other arithmetic  7.54 us (3%)
    pallas_call x1, Pallas kernels, line(): pl.pallas_call(functools.partial(line_kernel, sizes), out_shape=(jax.Shap...  85.3 us
    pallas_call x1, Pallas kernels, gather(): pl.pallas_call(functools.partial(gather_kernel, sizes), out_shape=(jax.Sh...  56.3 us
    pallas_call x1, Pallas kernels, exchange(): pl.pallas_call(functools.partial(table_kernel, sizes), out_shape=(jax.Sha...  27.3 us
    pallas_call x1, Pallas kernels, push(): pl.pallas_call(functools.partial(push_kernel, sizes), out_shape=jax.Shape...  17.9 us
    reduce_or x1, other arithmetic, body(): jnp.any(match, axis=2)  5.54 us

profile of v4, /device:TPU:0, one launch (start us, length us, event | category | flops | bytes accessed | tf_op | source)
XLA Modules:
  0.0 223.9 jit_solution(9963538247415392019)
XLA Ops:
  0.7 0.8 fusion.27
  1.6 0.7 select_reduce_fusion.1
  2.3 0.3 select_reduce_fusion
  2.7 0.6 pad.4.who_ref
  3.5 1.6 constant_dynamic-slice_fusion.qw_ref
  5.1 1.0 copy.30
  6.1 5.5 %fusion.1 = pred[128,4,256]{2,1,0:T(4,128)(4,1)S(1)} fusion(s32[128,4,32]{2,1,0:T(4,128)S(1)} %copy.30), kind=kLoop, calls=%fused_computation.2 | loop fusion | flops 8257536 | bytes 196608 | tf_op jit(solution)/shard_map/reduce_or | solution.py:522
  11.6 56.3 %gather_rows.1 = (bf16[4,2,2,2,2,64,512]{6,5,4,3,2,1,0:T(8,128)(2,1)}, bf16[4,256,512]{2,1,0:T(8,128)(2,1)}, bf16[3,8,128,512]{3,2,1,0:T(8,128)(2,1)}) custom-call(bf16[128,512]{1,0:T(8,128)(2,1)} %constant_dynamic-slice_fusion.qw_ref, bf16[256,4096]{1,0:T(8,128)(2,1)} %val_ref.1, bf16[128,4096]{1,0:T(8,128)(2,1)} %cot_ref.1), custom_call_target="tpu_custom_call" | custom-call | tf_op jit(solution)/shard_map/gather_rows/pallas_call | solution.py:413
  68.0 3.6 %convolution_convert_fusion = bf16[512,128]{1,0:T(8,128)(2,1)S(1)} fusion(bf16[4096,512]{1,0:T(8,128)(2,1)} %bitcast.50, bf16[128,4096]{1,0:T(8,128)(2,1)S(1)} %copy-done), kind=kOutput, calls=%fused_computation.20 | convolution fusion | flops 536936448 | bytes 5373952 | tf_op jit(solution)/shard_map/dot_general | solution.py:518
  71.6 0.5 fusion.30
  72.0 0.1 divide_convert_fusion
  72.2 0.2 copy.33
  72.5 1.2 fusion.15
  73.6 27.3 %exchange_tables.1 = (bf16[4,2,2,2,192,256]{5,4,3,2,1,0:T(8,128)(2,1)}, bf16[4,2,2,2,16,128]{5,4,3,2,1,0:T(8,128)(2,1)}) custom-call(bf16[4,192,256]{2,1,0:T(8,128)(2,1)} %bitcast.47, bf16[4,16,128]{2,1,0:T(8,128)(2,1)} %pad.4.who_ref), custom_call_target="tpu_custom_call" | custom-call | tf_op jit(solution)/shard_map/exchange_tables/pallas_call | solution.py:479
  100.9 0.9 slice.4
  101.9 3.7 %convert_bitcast_fusion = bf16[32,4,48,512]{3,2,0,1:T(8,128)(2,1)S(1)} fusion(bf16[32,4,48,256]{3,2,1,0:T(8,128)(2,1)} %bitcast.51, bf16[4,256,512]{2,1,0:T(8,128)(2,1)S(1)} %copy-done.3), kind=kOutput, calls=%fused_computation.3 | convolution fusion | flops 1613758464 | bytes 10485760 | tf_op jit(solution)/shard_map/dlcr,lrw->dlcw/dot_general | solution.py:553
  105.6 0.6 copy.35
  106.3 3.9 %fusion.10 = bf16[32,128,512]{2,1,0:T(8,128)(2,1)} fusion(bf16[32,192,512]{2,1,0:T(8,128)(2,1)S(1)} %bitcast.42, bf16[128]{0:T(256)(128)(2,1)S(1)} %iota_convert_fusion, bf16[32,192]{1,0:T(8,128)(2,1)S(1)} %eq.83), kind=kOutput, calls=%fused_computation.10 | convolution fusion | flops 808189952 | bytes 10498304 | tf_op jit(solution)/shard_map/dts,dsw->dtw/dot_general | solution.py:555
  110.1 85.3 %sum_line.1 = (bf16[128,4096]{1,0:T(8,128)(2,1)}, bf16[4,8,128,512]{3,2,1,0:T(8,128)(2,1)}) custom-call(bf16[4,8,128,512]{3,2,1,0:T(8,128)(2,1)} %bitcast.44, bf16[3,8,128,512]{3,2,1,0:T(8,128)(2,1)} %get-tuple-element.13.hop_ref), custom_call_target="tpu_custom_call" | custom-call | tf_op jit(solution)/shard_map/sum_line/pallas_call | solution.py:453
  195.4 4.5 %fusion.6 = bf16[32,192,512]{2,1,0:T(8,128)(2,1)S(1)} fusion(bf16[32,128,512]{2,1,0:T(8,128)(2,1)} %bitcast.45, bf16[128]{0:T(256)(128)(2,1)S(1)} %iota_convert_fusion, bf16[32,192]{1,0:T(8,128)(2,1)S(1)} %eq.83), kind=kOutput, calls=%fused_computation.8 | convolution fusion | flops 809238528 | bytes 10498304 | tf_op jit(solution)/shard_map/dts,dtw->dsw/dot_general | solution.py:560
  199.9 2.8 %bitcast_convert_fusion = bf16[4,256,512]{2,1,0:T(8,128)(2,1)} fusion(bf16[32,4,48,256]{3,2,1,0:T(8,128)(2,1)S(1)} %bitcast.52, bf16[32,4,48,512]{3,2,1,0:T(8,128)(2,1)S(1)} %bitcast.43), kind=kOutput, calls=%fused_computation.11 | convolution fusion | flops 1611137024 | bytes 10485760 | tf_op jit(solution)/shard_map/dlcr,dlcw->lrw/dot_general | solution.py:562
  202.7 17.9 %push_gradient.1 = bf16[128,4096]{1,0:T(8,128)(2,1)} custom-call(bf16[8,128,512]{2,1,0:T(8,128)(2,1)} %bitcast.46), custom_call_target="tpu_custom_call" | custom-call | tf_op jit(solution)/shard_map/push_gradient/pallas_call | solution.py:440
  220.7 1.0 copy.49
  221.6 2.3 %copy.50 = bf16[128,4096]{1,0:T(8,128)(2,1)} copy(bf16[128,4096]{1,0:T(8,128)(2,1)} %push_gradient.1) | data formatting | bytes 2097152
  (20 shorter events, 0.5 us)
Async XLA Ops:
  0.6 67.3 %copy-start = (bf16[128,4096]{1,0:T(8,128)(2,1)S(1)}, bf16[128,4096]{1,0:T(8,128)(2,1)}, u32[]{:S(2)}) copy-start(bf16[128,4096]{1,0:T(8,128)(2,1)} %param.7) | copy-start | bytes 3145732
  11.6 59.9 %copy-start.4 = (bf16[4,256,128]{2,1,0:T(8,128)(2,1)S(1)}, bf16[4,256,128]{2,1,0:T(8,128)(2,1)}, u32[]{:S(2)}) copy-start(bf16[4,256,128]{2,1,0:T(8,128)(2,1)} %param.11) | copy-start | bytes 786436
  68.0 33.9 %copy-start.3 = (bf16[4,256,512]{2,1,0:T(8,128)(2,1)S(1)}, bf16[4,256,512]{2,1,0:T(8,128)(2,1)}, u32[]{:S(2)}) copy-start(bf16[4,256,512]{2,1,0:T(8,128)(2,1)} %get-tuple-element.11) | copy-start | bytes 3145732
  195.4 4.5 %copy-start.2 = (bf16[4,2,2,2,192,256]{5,4,3,2,1,0:T(8,128)(2,1)S(1)}, bf16[4,2,2,2,192,256]{5,4,3,2,1,0:T(8,128)(2,1)}, u32[]{:S(2)}) copy-start(bf16[4,2,2,2,192,256]{5,4,3,2,1,0:T(8,128)(2,1)} %get-tuple-element.12) | copy-start | bytes 9437188
  199.9 20.7 %copy-start.1 = (bf16[128,4096]{1,0:T(8,128)(2,1)S(1)}, bf16[128,4096]{1,0:T(8,128)(2,1)}, u32[]{:S(2)}) copy-start(bf16[128,4096]{1,0:T(8,128)(2,1)} %get-tuple-element.22) | copy-start | bytes 3145732

commit v5 on v4

--- a/solution.py
+++ b/solution.py
@@ -162,24 +162,27 @@
         pl.when(z < far - 1)(lambda: hop(0).start())
         pl.when(z > 0)(lambda: hop(1).start())
 
+    pushes = []
+
+    def slices():
+        for number, step in enumerate(((0, 1, 0, 0), (0, 0, 1, 0), corner)):
+            peer = moved(me, sizes, step)
+            first = ((peer[1] * 2 + peer[2]) * sizes[3] + peer[3]) * part
+            copy = pltpu.make_async_remote_copy(
+                src_ref=val_ref.at[:, pl.ds(pl.multiple_of(first, part), part)],
+                dst_ref=vals_ref.at[me[1] * 2 + me[2]],
+                send_sem=vsend.at[number],
+                recv_sem=vrecv.at[number],
+                device_id=device(peer),
+                device_id_type=MESH,
+            )
+            copy.start()
+            pushes.append(copy)
+
     plans = [tree(order, sizes) for order in ORDERS]
-    events = ((1, cut), (12, forward))
+    events = ((1, cut), (12, forward), (14, slices))
     spread(me, sizes, plans, own, slot, started, send_sem, recv_sem, events)
     started.extend(cuts[:-1])
-    pushes = []
-    for number, step in enumerate(((0, 1, 0, 0), (0, 0, 1, 0), corner)):
-        peer = moved(me, sizes, step)
-        first = ((peer[1] * 2 + peer[2]) * sizes[3] + peer[3]) * part
-        copy = pltpu.make_async_remote_copy(
-            src_ref=val_ref.at[:, pl.ds(pl.multiple_of(first, part), part)],
-            dst_ref=vals_ref.at[me[1] * 2 + me[2]],
-            send_sem=vsend.at[number],
-            recv_sem=vrecv.at[number],
-            device_id=device(peer),
-            device_id_type=MESH,
-        )
-        copy.start()
-        pushes.append(copy)
     first = ((me[1] * 2 + me[2]) * sizes[3] + me[3]) * part
     vals_ref[me[1] * 2 + me[2]] = val_ref[:, pl.ds(pl.multiple_of(first, part), part)]
     for copy in started:

time: 224 us -> 224 us (level)
  no operation moved by 1% of the time
where the time goes in v5:
time: 224 us
  Pallas kernels  187 us (83%)
  matrix products  20.2 us (9%)
  local copies, waits for them, and re-layouts  8.54 us (4%)
  other arithmetic  7.54 us (3%)
    pallas_call x1, Pallas kernels, line(): pl.pallas_call(functools.partial(line_kernel, sizes), out_shape=(jax.Shap...  85.4 us
    pallas_call x1, Pallas kernels, gather(): pl.pallas_call(functools.partial(gather_kernel, sizes), out_shape=(jax.Sh...  56.3 us
    pallas_call x1, Pallas kernels, exchange(): pl.pallas_call(functools.partial(table_kernel, sizes), out_shape=(jax.Sha...  27.3 us
    pallas_call x1, Pallas kernels, push(): pl.pallas_call(functools.partial(push_kernel, sizes), out_shape=jax.Shape...  17.8 us
    reduce_or x1, other arithmetic, body(): jnp.any(match, axis=2)  5.54 us

profile of v5, /device:TPU:0, one launch (start us, length us, event | category | flops | bytes accessed | tf_op | source)
XLA Modules:
  0.0 223.9 jit_solution(973530285455304824)
XLA Ops:
  0.7 0.8 fusion.27
  1.6 0.7 select_reduce_fusion.1
  2.3 0.3 select_reduce_fusion
  2.7 0.6 pad.4.who_ref
  3.5 1.6 constant_dynamic-slice_fusion.qw_ref
  5.1 1.0 copy.30
  6.1 5.5 %fusion.1 = pred[128,4,256]{2,1,0:T(4,128)(4,1)S(1)} fusion(s32[128,4,32]{2,1,0:T(4,128)S(1)} %copy.30), kind=kLoop, calls=%fused_computation.2 | loop fusion | flops 8257536 | bytes 196608 | tf_op jit(solution)/shard_map/reduce_or | solution.py:525
  11.6 56.3 %gather_rows.1 = (bf16[4,2,2,2,2,64,512]{6,5,4,3,2,1,0:T(8,128)(2,1)}, bf16[4,256,512]{2,1,0:T(8,128)(2,1)}, bf16[3,8,128,512]{3,2,1,0:T(8,128)(2,1)}) custom-call(bf16[128,512]{1,0:T(8,128)(2,1)} %constant_dynamic-slice_fusion.qw_ref, bf16[256,4096]{1,0:T(8,128)(2,1)} %val_ref.1, bf16[128,4096]{1,0:T(8,128)(2,1)} %cot_ref.1), custom_call_target="tpu_custom_call" | custom-call | tf_op jit(solution)/shard_map/gather_rows/pallas_call | solution.py:416
  68.0 3.6 %convolution_convert_fusion = bf16[512,128]{1,0:T(8,128)(2,1)S(1)} fusion(bf16[4096,512]{1,0:T(8,128)(2,1)} %bitcast.50, bf16[128,4096]{1,0:T(8,128)(2,1)S(1)} %copy-done), kind=kOutput, calls=%fused_computation.20 | convolution fusion | flops 536936448 | bytes 5373952 | tf_op jit(solution)/shard_map/dot_general | solution.py:521
  71.6 0.5 fusion.30
  72.0 0.1 divide_convert_fusion
  72.2 0.2 copy.33
  72.5 1.2 fusion.15
  73.6 27.3 %exchange_tables.1 = (bf16[4,2,2,2,192,256]{5,4,3,2,1,0:T(8,128)(2,1)}, bf16[4,2,2,2,16,128]{5,4,3,2,1,0:T(8,128)(2,1)}) custom-call(bf16[4,192,256]{2,1,0:T(8,128)(2,1)} %bitcast.47, bf16[4,16,128]{2,1,0:T(8,128)(2,1)} %pad.4.who_ref), custom_call_target="tpu_custom_call" | custom-call | tf_op jit(solution)/shard_map/exchange_tables/pallas_call | solution.py:482
  100.9 0.9 slice.4
  101.9 3.7 %convert_bitcast_fusion = bf16[32,4,48,512]{3,2,0,1:T(8,128)(2,1)S(1)} fusion(bf16[32,4,48,256]{3,2,1,0:T(8,128)(2,1)} %bitcast.51, bf16[4,256,512]{2,1,0:T(8,128)(2,1)S(1)} %copy-done.3), kind=kOutput, calls=%fused_computation.3 | convolution fusion | flops 1613758464 | bytes 10485760 | tf_op jit(solution)/shard_map/dlcr,lrw->dlcw/dot_general | solution.py:556
  105.6 0.6 copy.35
  106.3 3.9 %fusion.10 = bf16[32,128,512]{2,1,0:T(8,128)(2,1)} fusion(bf16[32,192,512]{2,1,0:T(8,128)(2,1)S(1)} %bitcast.42, bf16[128]{0:T(256)(128)(2,1)S(1)} %iota_convert_fusion, bf16[32,192]{1,0:T(8,128)(2,1)S(1)} %eq.83), kind=kOutput, calls=%fused_computation.10 | convolution fusion | flops 808189952 | bytes 10498304 | tf_op jit(solution)/shard_map/dts,dsw->dtw/dot_general | solution.py:558
  110.1 85.4 %sum_line.1 = (bf16[128,4096]{1,0:T(8,128)(2,1)}, bf16[4,8,128,512]{3,2,1,0:T(8,128)(2,1)}) custom-call(bf16[4,8,128,512]{3,2,1,0:T(8,128)(2,1)} %bitcast.44, bf16[3,8,128,512]{3,2,1,0:T(8,128)(2,1)} %get-tuple-element.13.hop_ref), custom_call_target="tpu_custom_call" | custom-call | tf_op jit(solution)/shard_map/sum_line/pallas_call | solution.py:456
  195.5 4.5 %fusion.6 = bf16[32,192,512]{2,1,0:T(8,128)(2,1)S(1)} fusion(bf16[32,128,512]{2,1,0:T(8,128)(2,1)} %bitcast.45, bf16[128]{0:T(256)(128)(2,1)S(1)} %iota_convert_fusion, bf16[32,192]{1,0:T(8,128)(2,1)S(1)} %eq.83), kind=kOutput, calls=%fused_computation.8 | convolution fusion | flops 809238528 | bytes 10498304 | tf_op jit(solution)/shard_map/dts,dtw->dsw/dot_general | solution.py:563
  200.0 2.8 %bitcast_convert_fusion = bf16[4,256,512]{2,1,0:T(8,128)(2,1)} fusion(bf16[32,4,48,256]{3,2,1,0:T(8,128)(2,1)S(1)} %bitcast.52, bf16[32,4,48,512]{3,2,1,0:T(8,128)(2,1)S(1)} %bitcast.43), kind=kOutput, calls=%fused_computation.11 | convolution fusion | flops 1611137024 | bytes 10485760 | tf_op jit(solution)/shard_map/dlcr,dlcw->lrw/dot_general | solution.py:565
  202.8 17.8 %push_gradient.1 = bf16[128,4096]{1,0:T(8,128)(2,1)} custom-call(bf16[8,128,512]{2,1,0:T(8,128)(2,1)} %bitcast.46), custom_call_target="tpu_custom_call" | custom-call | tf_op jit(solution)/shard_map/push_gradient/pallas_call | solution.py:443
  220.7 1.0 copy.49
  221.6 2.3 %copy.50 = bf16[128,4096]{1,0:T(8,128)(2,1)} copy(bf16[128,4096]{1,0:T(8,128)(2,1)} %push_gradient.1) | data formatting | bytes 2097152
  (20 shorter events, 0.5 us)
Async XLA Ops:
  0.6 67.3 %copy-start = (bf16[128,4096]{1,0:T(8,128)(2,1)S(1)}, bf16[128,4096]{1,0:T(8,128)(2,1)}, u32[]{:S(2)}) copy-start(bf16[128,4096]{1,0:T(8,128)(2,1)} %param.7) | copy-start | bytes 3145732
  11.6 59.9 %copy-start.4 = (bf16[4,256,128]{2,1,0:T(8,128)(2,1)S(1)}, bf16[4,256,128]{2,1,0:T(8,128)(2,1)}, u32[]{:S(2)}) copy-start(bf16[4,256,128]{2,1,0:T(8,128)(2,1)} %param.11) | copy-start | bytes 786436
  68.0 33.9 %copy-start.3 = (bf16[4,256,512]{2,1,0:T(8,128)(2,1)S(1)}, bf16[4,256,512]{2,1,0:T(8,128)(2,1)}, u32[]{:S(2)}) copy-start(bf16[4,256,512]{2,1,0:T(8,128)(2,1)} %get-tuple-element.11) | copy-start | bytes 3145732
  195.5 4.5 %copy-start.2 = (bf16[4,2,2,2,192,256]{5,4,3,2,1,0:T(8,128)(2,1)S(1)}, bf16[4,2,2,2,192,256]{5,4,3,2,1,0:T(8,128)(2,1)}, u32[]{:S(2)}) copy-start(bf16[4,2,2,2,192,256]{5,4,3,2,1,0:T(8,128)(2,1)} %get-tuple-element.12) | copy-start | bytes 9437188
  200.0 20.7 %copy-start.1 = (bf16[128,4096]{1,0:T(8,128)(2,1)S(1)}, bf16[128,4096]{1,0:T(8,128)(2,1)}, u32[]{:S(2)}) copy-start(bf16[128,4096]{1,0:T(8,128)(2,1)} %get-tuple-element.22) | copy-start | bytes 3145732
